TPU v7x, 256 devices: a whole 4x4x8 slice. The times are simulated.
256 devices in a mesh: frame: 8 (over x, core), cell: 32 (over z, y).
Axes of the slice: x: 4, y: 4, z: 8, core: 2. Of those that a mesh axis runs over, the one named last changes fastest.
Arguments:
- a_blocks: bfloat16 [4096, 64, 384], P(('frame', 'cell')), may hold values from -0.3125 to 0.3125
- a_cols: int32 [4096, 6], P(('frame', 'cell')), may hold values from 0 to 4095, as said below
- p_blocks: bfloat16 [4096, 64, 128], P(('frame', 'cell')), may hold values from -2 to 2
- p_cells: int32 [4096, 2], P(('frame', 'cell')), may hold values from 0 to 31, all different within a row; in each aligned block of 16 rows (0 to 15, 16 to 31, ...) at most 2 rows name the same one
Outputs:
- coarse_blocks: bfloat16 [512, 3, 3, 64, 2048], P(('frame', 'cell'))
Inputs may be any that keep to these rules, and one draw needn't show every extreme that they name: a_cols[g, 0] = g. Every other stored block names a fine row of the same cell group, in the same or an adjacent frame range, whose local row differs from g's by at most 8; at most one of them lies in the previous and at most one in the next frame range. `p_cells`: the cells named in one row differ. Among the rows of one device, no cell is named more than 2 times, a bound that some block reaches.
All inputs are finite; a program needn't handle non-finite values.
Results may differ from a plain program's by a relative error of at most 0.0049.
Values may be sent and summed in bfloat16 or wider, within the bound.
No kernel may reach another device: no remote copies, remote signals or barrier semaphores. Data moves between devices by JAX's collectives and lax.ppermute only.
A program may use at most 192 MiB of HBM per device.

v0:
```python
import jax
import jax.numpy as jnp
from jax import lax
from jax.sharding import PartitionSpec as P

AGG = 8


def extended(value, sides, width):
    for axis, dim in sides:
        count, length = (lax.axis_size(axis), value.shape[dim])
        up = [(i, (i + 1) % count) for i in range(count - 1)]
        down = [(j, i) for i, j in up]
        last = lax.slice_in_dim(value, length - width, length, axis=dim)
        initial = lax.slice_in_dim(value, 0, width, axis=dim)
        before = lax.ppermute(last, axis, up)
        after = lax.ppermute(initial, axis, down)
        value = jnp.concatenate([before, value, after], axis=dim)
    return value


def for_sending(value):
    return jax.tree.map(lambda a: a.astype(jnp.bfloat16) if a.dtype == jnp.float32 else a, value)


def local(a_blocks, a_cols, p_blocks, p_cells):
    rows = a_blocks.shape[0]
    width = a_blocks.shape[1]
    nnz_a = a_blocks.shape[2] // width
    nnz_p = p_blocks.shape[2] // width
    lanes = nnz_p * width
    cells = lax.axis_size("cell")
    frame = lax.axis_index("frame")
    coarse_here = rows // AGG
    segments = coarse_here * 9
    capacity = min(rows, 2 * rows * nnz_p // cells)
    near_blocks, near_cells = (
        extended(p_blocks, (("frame", 0),), rows),
        extended(p_cells, (("frame", 0),), rows),
    )
    a_four = a_blocks.reshape(rows, width, nnz_a, width)
    offset_u = a_cols // (rows * cells) - frame + 1
    place_far = offset_u * rows + a_cols % rows
    p_far = near_blocks[place_far]
    cell_far = near_cells[place_far]
    products = jnp.einsum(
        "iakb,ikbn->ikan", a_four, p_far, preferred_element_type=jnp.float32
    ).astype(jnp.bfloat16)
    local_agg = jnp.arange(rows, dtype=jnp.int32) // AGG
    offset_v = a_cols % rows // AGG - local_agg[:, None] + 1
    seg_index = local_agg[:, None] * 9 + offset_u * 3 + offset_v
    seg_full = jnp.broadcast_to(seg_index[:, :, None], (rows, nnz_a, nnz_p))
    target = jnp.stack([seg_full, cell_far], axis=-1)
    slot_cells = p_cells.reshape(-1)
    onehot = (slot_cells[:, None] == jnp.arange(cells, dtype=jnp.int32)[None, :]).astype(jnp.int32)
    place = jnp.sum((jnp.cumsum(onehot, 0) - onehot) * onehot, 1)
    source = (
        jnp.full((cells, capacity), rows * nnz_p, jnp.int32)
        .at[slot_cells, place]
        .set(jnp.arange(rows * nnz_p, dtype=jnp.int32))
    )
    source_row = source // nnz_p
    source_slot = source % nnz_p
    target_buffer = target.at[source_row].get(mode="fill", fill_value=0)
    product_buffer = products.at[source_row].get(mode="fill", fill_value=0)
    p_rows = p_blocks.at[source_row].get(mode="fill", fill_value=0)
    keep_lane = (
        jnp.arange(lanes, dtype=jnp.int32)[None, None, None, :] // width
        == source_slot[:, :, None, None]
    )
    p_masked = jnp.where(keep_lane, p_rows, jnp.zeros_like(p_rows))
    got_p, got_products, got_targets = (
        lax.all_to_all(p_masked, "cell", split_axis=0, concat_axis=0, tiled=True),
        lax.all_to_all(product_buffer, "cell", split_axis=0, concat_axis=0, tiled=True),
        lax.all_to_all(
            for_sending(target_buffer), "cell", split_axis=0, concat_axis=0, tiled=True
        ).astype(target_buffer.dtype),
    )
    full_terms = jnp.einsum(
        "csbm,cskbn->cskmn", got_p, got_products, preferred_element_type=jnp.float32
    )
    terms = full_terms.reshape(cells, capacity, nnz_a, nnz_p, width, lanes).sum(3)
    updates = terms.reshape(cells, capacity, nnz_a, width, nnz_p, width)
    numbers = lax.ScatterDimensionNumbers(
        update_window_dims=(3, 5), inserted_window_dims=(0, 2), scatter_dims_to_operand_dims=(0, 2)
    )
    summed = jnp.zeros((segments, width, cells, width), jnp.float32)
    summed = lax.scatter_add(summed, got_targets, updates, numbers)
    return summed.reshape(coarse_here, 3, 3, width, cells * width).astype(jnp.bfloat16)


def solution(mesh):
    placed = (
        P(("frame", "cell"), None, None),
        P(("frame", "cell"), None),
        P(("frame", "cell"), None, None),
        P(("frame", "cell"), None),
    )
    return jax.shard_map(
        local,
        mesh=mesh,
        in_specs=placed,
        out_specs=P(("frame", "cell"), None, None, None, None),
        check_vma=False,
    )
```

profile of v0, /device:TPU:9, one launch (start us, length us, event | category | flops | bytes accessed | tf_op | source)
XLA Modules:
  0.0 472.8 jit_solution(14989674391714649769)
XLA Ops:
  0.0 3.8 collective-permute-start
  3.8 1.9 collective-permute-start.1
  7.1 2.0 scatter_fusion
  15.6 11.1 %all-to-all-start = ((s32[32,2,6,2,2]{2,4,3,1,0:T(2,128)}), s32[32,2,6,2,2]{2,4,3,1,0:T(2,128)S(1)}, u32[]{:S(2)}, u32[]{:S(2)}) async-start(s32[32,2,6,2,2]{2,4,3,1,0:T(2,128)} %broadcast_select_fusion.1), calls=%async_computation | async-start | bytes 262144 | tf_op jit(solution)/shard_map/all_to_all | solution.py:75
  28.0 6.9 %all-to-all-done = s32[32,2,6,2,2]{2,4,3,1,0:T(2,128)S(1)} async-done(((s32[32,2,6,2,2]{2,4,3,1,0:T(2,128)}), s32[32,2,6,2,2]{2,4,3,1,0:T(2,128)S(1)}, u32[]{:S(2)}, u32[]{:S(2)}) %all-to-all-start) | async-done | bytes 6176 | tf_op jit(solution)/shard_map/all_to_all | solution.py:75
  34.9 5.9 %all-to-all-start.2 = ((bf16[32,2,64,128]{3,2,1,0:T(8,128)(2,1)}), bf16[32,2,64,128]{3,2,1,0:T(8,128)(2,1)}, u32[]{:S(2)}, u32[]{:S(2)}) async-start(bf16[32,2,64,128]{3,2,1,0:T(8,128)(2,1)} %select_select_fusion), calls=%async_computation.2 | async-start | bytes 2097152 | tf_op jit(solution)/shard_map/all_to_all | solution.py:73
  40.8 1.9 collective-permute-start.3
  42.8 5.1 %collective-permute-start.2 = (bf16[16,64,128]{2,1,0:T(8,128)(2,1)S(1)}, bf16[16,64,128]{2,1,0:T(8,128)(2,1)S(1)}, u32[]{:S(2)}, u32[]{:S(2)}) collective-permute-start(bf16[16,64,128]{2,1,0:T(8,128)(2,1)S(1)} %copy-done), channel_id=1, source_target_pairs={{0,32},{32,64},{64,96},{96,128},{128,160},{160,192},{192,224},{1,3... | collective-permute-start | bytes 786440 | tf_op jit(solution)/shard_map/ppermute | solution.py:16
  47.9 2.1 reshape.123
  52.1 2.1 fusion.1
  54.2 4.0 gather_fusion.3
  58.3 5.9 %broadcast_select_fusion = bf16[32,2,6,64,128]{4,3,2,1,0:T(8,128)(2,1)} fusion(bf16[32,2,6,64,128]{4,3,2,1,0:T(8,128)(2,1)} %bitcast.36, pred[32,2]{1,0:T(8,128)(4,1)S(1)} %copy.70), kind=kLoop, calls=%fused_computation.7 | loop fusion | flops 3145728 | bytes 12582976 | tf_op jit(solution)/shard_map/select_n | solution.py:65
  64.2 5.4 %all-to-all-done.2 = bf16[32,2,64,128]{3,2,1,0:T(8,128)(2,1)} async-done(((bf16[32,2,64,128]{3,2,1,0:T(8,128)(2,1)}), bf16[32,2,64,128]{3,2,1,0:T(8,128)(2,1)}, u32[]{:S(2)}, u32[]{:S(2)}) %all-to-all-start.2) | async-done | bytes 1048608 | tf_op jit(solution)/shard_map/all_to_all | solution.py:73
  69.6 4.9 %all-to-all-start.1 = ((bf16[32,2,6,64,128]{4,3,2,1,0:T(8,128)(2,1)}), bf16[32,2,6,64,128]{4,3,2,1,0:T(8,128)(2,1)}, u32[]{:S(2)}, u32[]{:S(2)}) async-start(bf16[32,2,6,64,128]{4,3,2,1,0:T(8,128)(2,1)} %broadcast_select_fusion), calls=%async_computation.1 | async-start | bytes 12582912 | tf_op jit(solution)/shard_map/all_to_all | solution.py:74
  75.4 143.2 %all-to-all-done.1 = bf16[32,2,6,64,128]{4,3,2,1,0:T(8,128)(2,1)} async-done(((bf16[32,2,6,64,128]{4,3,2,1,0:T(8,128)(2,1)}), bf16[32,2,6,64,128]{4,3,2,1,0:T(8,128)(2,1)}, u32[]{:S(2)}, u32[]{:S(2)}) %all-to-all-start.1) | async-done | bytes 6291488 | tf_op jit(solution)/shard_map/all_to_all | solution.py:74
  218.6 14.8 %fusion.4 = f32[32,2,6,128,128]{3,4,2,1,0:T(8,128)} fusion(bf16[32,2,6,64,128]{4,3,2,1,0:T(8,128)(2,1)} %all-to-all-done.1, bf16[32,2,64,128]{3,2,1,0:T(8,128)(2,1)} %all-to-all-done.2), kind=kOutput, calls=%fused_computation.11 | convolution fusion | flops 805306368 | bytes 32505856 | tf_op jit(solution)/shard_map/csbm,cskbn->cskmn/dot_general | solution.py:79
  233.4 15.1 %reduce_sum.22 = f32[32,2,6,64,128]{4,3,2,1,0:T(8,128)} reduce(f32[32,2,6,2,64,128]{5,4,3,2,1,0:T(8,128)} %bitcast.35, f32[]{:T(128)} %constant.112.clone.1), dimensions={3}, to_apply=%region_3.4 | reduce | flops 3145728 | bytes 37748740 | tf_op jit(solution)/shard_map/reduce_sum | solution.py:82
  248.5 24.6 %reshape.125 = f32[32,2,6,64,2,64]{5,4,3,2,1,0:T(2,128)} reshape(f32[32,2,6,64,128]{4,3,2,1,0:T(8,128)} %reduce_sum.22) | data formatting | bytes 25165824 | tf_op jit(solution)/shard_map/reshape | solution.py:83
  273.1 19.0 %copy.82 = f32[32,2,6,2,64,64]{5,4,3,2,1,0:T(8,128)} copy(f32[32,2,6,2,64,64]{5,3,4,2,1,0:T(2,128)} %bitcast.33) | data formatting | bytes 25165824 | tf_op jit(solution)/shard_map/reshape | solution.py:83
  292.1 8.9 %broadcast_in_dim.46 = f32[18,64,32,64]{3,1,2,0:T(8,128)} broadcast(f32[]{:T(128)} %constant.112.clone.1), dimensions={} | broadcast | bytes 9437188 | tf_op jit(solution)/shard_map/broadcast_in_dim | solution.py:87
  301.0 132.2 %scatter_fusion.1 = f32[18,64,32,64]{3,1,2,0:T(8,128)} fusion(f32[18,64,32,64]{3,1,2,0:T(8,128)} %broadcast_in_dim.46, s32[768]{0:T(1024)S(1)} %reshape.172, f32[768,64,64]{2,1,0:T(8,128)} %bitcast.34), kind=kCustom, calls=%fused_computation.6 | custom fusion | flops 3145728 | bytes 37754880 | tf_op jit(solution)/shard_map/scatter-add | solution.py:88
  433.2 10.3 %convert_element_type.18 = bf16[18,64,32,64]{3,1,2,0:T(8,128)(2,1)} convert(f32[18,64,32,64]{3,1,2,0:T(8,128)} %scatter_fusion.1) | non-fusion elementwise | flops 2359296 | bytes 14155776 | tf_op jit(solution)/shard_map/convert_element_type | solution.py:89
  443.5 15.4 %copy.83 = bf16[18,64,32,64]{3,2,1,0:T(8,128)(2,1)} copy(bf16[18,64,32,64]{3,1,2,0:T(8,128)(2,1)} %convert_element_type.18) | data formatting | bytes 9437184 | tf_op jit(solution)/shard_map/convert_element_type | solution.py:89
  459.0 13.8 %convert_element_type.19 = bf16[2,3,3,64,2048]{4,3,2,1,0:T(8,128)(2,1)} reshape(bf16[18,64,32,64]{3,2,1,0:T(8,128)(2,1)} %copy.83) | data formatting | bytes 9437184 | tf_op jit(solution)/shard_map/convert_element_type | solution.py:89
  (49 shorter events, 11.9 us)
Async XLA Ops:
  0.0 40.8 %copy-start = (bf16[16,64,128]{2,1,0:T(8,128)(2,1)S(1)}, bf16[16,64,128]{2,1,0:T(8,128)(2,1)}, u32[]{:S(2)}) copy-start(bf16[16,64,128]{2,1,0:T(8,128)(2,1)} %param.6) | copy-start | bytes 786436
  0.0 47.8 %copy-start.1 = (bf16[16,64,384]{2,1,0:T(8,128)(2,1)S(1)}, bf16[16,64,384]{2,1,0:T(8,128)(2,1)}, u32[]{:S(2)}) copy-start(bf16[16,64,384]{2,1,0:T(8,128)(2,1)} %param.4) | copy-start | bytes 2359300
  0.0 12.3 %collective-permute-start = (s32[16,2]{0,1:T(2,128)}, s32[16,2]{0,1:T(2,128)S(1)}, u32[]{:S(2)}, u32[]{:S(2)}) collective-permute-start(s32[16,2]{0,1:T(2,128)} %param.7), channel_id=1, source_target_pairs={{0,32},{32,64},{64,96},{96,128},{128,160},{160,192},{192,224},{1,3... | collective-permute-start | bytes 392 | tf_op jit(solution)/shard_map/ppermute | solution.py:16
  3.8 8.5 %collective-permute-start.1 = (s32[16,2]{0,1:T(2,128)}, s32[16,2]{0,1:T(2,128)S(1)}, u32[]{:S(2)}, u32[]{:S(2)}) collective-permute-start(s32[16,2]{0,1:T(2,128)} %param.7), channel_id=1, source_target_pairs={{32,0},{64,32},{96,64},{128,96},{160,128},{192,160},{224,192},{33,... | collective-permute-start | bytes 392 | tf_op jit(solution)/shard_map/ppermute | solution.py:17
  15.6 19.3 %all-to-all-start = ((s32[32,2,6,2,2]{2,4,3,1,0:T(2,128)}), s32[32,2,6,2,2]{2,4,3,1,0:T(2,128)S(1)}, u32[]{:S(2)}, u32[]{:S(2)}) async-start(s32[32,2,6,2,2]{2,4,3,1,0:T(2,128)} %broadcast_select_fusion.1), calls=%async_computation | async-start | bytes 262144 | tf_op jit(solution)/shard_map/all_to_all | solution.py:75
  34.9 34.7 %all-to-all-start.2 = ((bf16[32,2,64,128]{3,2,1,0:T(8,128)(2,1)}), bf16[32,2,64,128]{3,2,1,0:T(8,128)(2,1)}, u32[]{:S(2)}, u32[]{:S(2)}) async-start(bf16[32,2,64,128]{3,2,1,0:T(8,128)(2,1)} %select_select_fusion), calls=%async_computation.2 | async-start | bytes 2097152 | tf_op jit(solution)/shard_map/all_to_all | solution.py:73
  40.8 9.5 %collective-permute-start.3 = (bf16[16,64,128]{2,1,0:T(8,128)(2,1)S(1)}, bf16[16,64,128]{2,1,0:T(8,128)(2,1)S(1)}, u32[]{:S(2)}, u32[]{:S(2)}) collective-permute-start(bf16[16,64,128]{2,1,0:T(8,128)(2,1)S(1)} %copy-done), channel_id=1, source_target_pairs={{32,0},{64,32},{96,64},{128,96},{160,128},{192,160},{224,192},{33,... | collective-permute-start | bytes 786440 | tf_op jit(solution)/shard_map/ppermute | solution.py:17
  42.8 8.4 %collective-permute-start.2 = (bf16[16,64,128]{2,1,0:T(8,128)(2,1)S(1)}, bf16[16,64,128]{2,1,0:T(8,128)(2,1)S(1)}, u32[]{:S(2)}, u32[]{:S(2)}) collective-permute-start(bf16[16,64,128]{2,1,0:T(8,128)(2,1)S(1)} %copy-done), channel_id=1, source_target_pairs={{0,32},{32,64},{64,96},{96,128},{128,160},{160,192},{192,224},{1,3... | collective-permute-start | bytes 786440 | tf_op jit(solution)/shard_map/ppermute | solution.py:16
  69.6 149.0 %all-to-all-start.1 = ((bf16[32,2,6,64,128]{4,3,2,1,0:T(8,128)(2,1)}), bf16[32,2,6,64,128]{4,3,2,1,0:T(8,128)(2,1)}, u32[]{:S(2)}, u32[]{:S(2)}) async-start(bf16[32,2,6,64,128]{4,3,2,1,0:T(8,128)(2,1)} %broadcast_select_fusion), calls=%async_computation.1 | async-start | bytes 12582912 | tf_op jit(solution)/shard_map/all_to_all | solution.py:74
where the time goes:
time: 478 us; the launch traced here: 473 us
  other arithmetic  168 us (35%)
  waiting for transfers between devices  157 us (33%)
  local copies, waits for them, and re-layouts  96.2 us (20%)
  starting transfers between devices  34.7 us (7%)
  matrix products  16.9 us (4%)
    all_to_all x1, waiting for transfers between devices, local(): lax.all_to_all(product_buffer, 'cell', split_axis=0, concat_axis=0, tiled...  143 us
    scatter-add x1, other arithmetic, local(): summed = lax.scatter_add(summed, got_targets, updates, numbers)  132 us
    reshape x2, local copies, waits for them, and re-layouts, local(): updates = terms.reshape(cells, capacity, nnz_a, width, nnz_p, width)  43.6 us
    convert_element_type x2, local copies, waits for them, and re-layouts, local(): summed.reshape(coarse_here, 3, 3, width, cells * width).astype(jnp.bfloat16)  29.2 us
    reduce_sum x1, other arithmetic, local(): full_terms.reshape(cells, capacity, nnz_a, nnz_p, width, lanes).sum(3)  15.1 us
    dot_general x1, matrix products, local(): jnp.einsum('csbm,cskbn->cskmn', got_p, got_products, preferred_element_ty...  14.8 us
    all_to_all x1, starting transfers between devices, local(): lax.all_to_all(for_sending(target_buffer), 'cell', split_axis=0, concat_a...  11.1 us
    convert_element_type x1, other arithmetic, local(): summed.reshape(coarse_here, 3, 3, width, cells * width).astype(jnp.bfloat16)  10.3 us
  transfers between devices with their start and end apart: 7, of which 5 were waited for; matrix products, arithmetic and copies ran while one was open for 5% of the time, Pallas kernels for 0%

commit v1 on v0

v1 whole, which is shorter than its diff:
```python
import functools

import jax
import jax.numpy as jnp
from jax import lax
from jax.experimental import pallas as pl
from jax.experimental.pallas import tpu as pltpu
from jax.sharding import PartitionSpec as P

AGG = 8
BS = 64


def shifted(value, axis):
    n = lax.axis_size(axis)
    up = [(i, i + 1) for i in range(n - 1)]
    down = [(i + 1, i) for i in range(n - 1)]
    return lax.ppermute(value, axis, up), lax.ppermute(value, axis, down)


def send_kernel(rows, nnz_a, meta, a_ref, pb, pm, pa, out, pall, apbuf, tbuf, count, psem, sems):
    copies = [
        pltpu.make_async_copy(src, pall.at[pl.ds(i * rows, rows)], psem.at[i])
        for i, src in enumerate((pb, pm, pa))
    ]
    for c in copies:
        c.start()

    def clear(i, _):
        count[i] = 0
        return 0

    lax.fori_loop(0, count.shape[0], clear, 0)
    for c in copies:
        c.wait()
    zero = jnp.zeros((BS, 2 * BS), jnp.bfloat16)

    def row(r, _):
        for m in range(nnz_a // 2):
            f0 = meta[r * 8 + 2 * m] & 63
            f1 = meta[r * 8 + 2 * m + 1] & 63
            rhs = jnp.concatenate(
                [
                    jnp.concatenate([pall[f0], zero], axis=1),
                    jnp.concatenate([zero, pall[f1]], axis=1),
                ],
                axis=0,
            )
            ap = jnp.dot(
                a_ref[r, :, 2 * BS * m : 2 * BS * (m + 1)], rhs, preferred_element_type=jnp.float32
            )
            apbuf[r, :, 4 * BS * m : 4 * BS * (m + 1)] = ap.astype(jnp.bfloat16)
        t = lax.dot_general(
            pall[rows + r], apbuf[r], (((0,), (0,)), ((), ())), preferred_element_type=jnp.float32
        )
        tbuf[r] = t.astype(jnp.bfloat16)
        for p in range(2):
            c = meta[r * 8 + 6 + p]
            place = count[c]
            count[c] = place + 1
            pltpu.make_async_copy(
                tbuf.at[r, pl.ds(p * BS, BS)],
                out.at[c, pl.ds(pl.multiple_of(place * BS, BS), BS)],
                sems.at[r * 2 + p],
            ).start()
        return 0

    lax.fori_loop(0, rows, row, 0, unroll=2)

    def finish(i, _):
        pltpu.make_async_copy(tbuf.at[0, pl.ds(0, BS)], out.at[0, pl.ds(0, BS)], sems.at[i]).wait()
        return 0

    lax.fori_loop(0, 2 * rows, finish, 0)


def add_kernel(nseg, cells, nnz_a, per, meta, slots, got, out, acc, stage, sems):
    i = pl.program_id(0)

    @pl.when(i == 0)
    def _():
        def clear(j, _):
            acc[pl.ds(j * 4, 4)] = jnp.zeros((4,) + acc.shape[1:], jnp.float32)
            return 0

        lax.fori_loop(0, acc.shape[0] // 4, clear, 0)

    low = lax.broadcasted_iota(jnp.int32, (BS, 2 * BS), 1) < BS

    def slot(j, _):
        s = i * per + j
        e = slots[s]

        @pl.when(e >= 0)
        def _():
            c = s // 2
            base = cells * 128 + c * 128 + (e // 2) * 8
            for k in range(nnz_a):
                w = meta[base + k]
                far = w & 63
                seg = w >> 6
                src = (far >> 4) * (cells * 128) + c * 128 + (far & 15) * 8 + 6
                i0 = seg * cells + meta[src]
                i1 = seg * cells + meta[src + 1]
                x = got[j, :, 2 * BS * k : 2 * BS * (k + 1)].astype(jnp.float32)
                new0 = acc[i0] + jnp.where(low, x, 0.0)
                new1 = acc[i1] + jnp.where(low, 0.0, x)
                acc[i0] = new0
                acc[i1] = new1

        return 0

    lax.fori_loop(0, per, slot, 0)

    @pl.when(i == pl.num_programs(0) - 1)
    def _():
        def put(seg, _):
            for h in range(cells // 2):
                a = acc[seg * cells + 2 * h]
                b = acc[seg * cells + 2 * h + 1]
                v = jnp.where(low, a, b) + pltpu.roll(jnp.where(low, b, a), BS, 1)
                stage[seg, :, 2 * BS * h : 2 * BS * (h + 1)] = v.astype(jnp.bfloat16)
            pltpu.make_async_copy(stage.at[seg], out.at[seg], sems.at[seg]).start()
            return 0

        lax.fori_loop(0, nseg, put, 0)

        def finish(seg, _):
            pltpu.make_async_copy(stage.at[seg], out.at[seg], sems.at[seg]).wait()
            return 0

        lax.fori_loop(0, nseg, finish, 0)


def local(a_blocks, a_cols, p_blocks, p_cells):
    rows = a_blocks.shape[0]
    nnz_a = a_cols.shape[1]
    cells = lax.axis_size("cell")
    frame = lax.axis_index("frame")
    me = lax.axis_index("cell")
    coarse_here = rows // AGG
    nseg = coarse_here * 9

    before, after = shifted(p_blocks, "frame")
    where_u = lax.div(a_cols, jnp.int32(rows * cells)) - frame + 1
    where_r = a_cols & (rows - 1)
    agg = jnp.arange(rows, dtype=jnp.int32)[:, None] // AGG
    seg = agg * 9 + where_u * 3 + where_r // AGG - agg + 1
    meta = jnp.concatenate([where_u * rows + where_r + 64 * seg, p_cells], axis=1).reshape(rows * 8)
    everyone = lax.all_to_all(
        jnp.broadcast_to(meta[None], (cells, rows * 8)), "cell", 0, 0, tiled=True
    )
    mb, ma = shifted(everyone, "frame")
    three = jnp.stack([mb, everyone, ma]).reshape(-1)
    named = everyone.reshape(cells, rows, 8)[:, :, 6:].reshape(cells, 2 * rows)
    entry = jnp.arange(2 * rows, dtype=jnp.int32)[None]
    hit = named == me
    first = jnp.min(jnp.where(hit, entry, 2 * rows), axis=1)
    last = jnp.max(jnp.where(hit, entry, -1), axis=1)
    slots = jnp.stack(
        [jnp.where(first < 2 * rows, first, -1), jnp.where(last > first, last, -1)], axis=1
    ).reshape(2 * cells)

    wide = 2 * nnz_a * BS
    any_spec = pl.BlockSpec(memory_space=pl.ANY)
    smem = pl.BlockSpec(memory_space=pltpu.SMEM)
    buffer = pl.pallas_call(
        functools.partial(send_kernel, rows, nnz_a),
        out_shape=jax.ShapeDtypeStruct((cells, 2 * BS, wide), jnp.bfloat16),
        in_specs=[smem, pl.BlockSpec(memory_space=pltpu.VMEM), any_spec, any_spec, any_spec],
        out_specs=any_spec,
        scratch_shapes=[
            pltpu.VMEM((3 * rows, BS, 2 * BS), jnp.bfloat16),
            pltpu.VMEM((rows, BS, wide), jnp.bfloat16),
            pltpu.VMEM((rows, 2 * BS, wide), jnp.bfloat16),
            pltpu.SMEM((cells,), jnp.int32),
            pltpu.SemaphoreType.DMA((3,)),
            pltpu.SemaphoreType.DMA((2 * rows,)),
        ],
        name="send",
    )(meta, a_blocks, before, p_blocks, after)
    got = lax.all_to_all(buffer, "cell", 0, 0, tiled=True).reshape(2 * cells, BS, wide)
    per = 8
    out = pl.pallas_call(
        functools.partial(add_kernel, nseg, cells, nnz_a, per),
        out_shape=jax.ShapeDtypeStruct((nseg, BS, cells * BS), jnp.bfloat16),
        grid=(2 * cells // per,),
        in_specs=[smem, smem, pl.BlockSpec((per, BS, wide), lambda i: (i, 0, 0))],
        out_specs=any_spec,
        scratch_shapes=[
            pltpu.VMEM((nseg * cells, BS, 2 * BS), jnp.float32),
            pltpu.VMEM((nseg, BS, cells * BS), jnp.bfloat16),
            pltpu.SemaphoreType.DMA((nseg,)),
        ],
        compiler_params=pltpu.CompilerParams(vmem_limit_bytes=50 << 20),
        name="add",
    )(three, slots, got)
    return out.reshape(coarse_here, 3, 3, BS, cells * BS)


def solution(mesh):
    placed = (
        P(("frame", "cell"), None, None),
        P(("frame", "cell"), None),
        P(("frame", "cell"), None, None),
        P(("frame", "cell"), None),
    )
    return jax.shard_map(
        local,
        mesh=mesh,
        in_specs=placed,
        out_specs=P(("frame", "cell"), None, None, None, None),
        check_vma=False,
    )
```

time: 478 us -> 198 us (0.41)
  other arithmetic: 168 us -> 1.54 us
  local copies, waits for them, and re-layouts: 96.2 us -> 2.44 us
  Pallas kernels: 0 us -> 20.3 us
  waiting for transfers between devices: 157 us -> 139 us
  matrix products: 16.9 us -> 0 us
    scatter-add x1 -> x0, other arithmetic: 132 us -> none  [local(): summed = lax.scatter_add(summed, got_targets, updates, numbers)]
    reshape x4 -> x1, local copies, waits for them, and re-layouts: 45.8 us -> 0.1 us  [local(): slots = jnp.stack([jnp.where(first < 2 * rows, first, -1), jnp.where(last...]
    convert_element_type x2 -> x0, local copies, waits for them, and re-layouts: 29.2 us -> none  [local(): summed.reshape(coarse_here, 3, 3, width, cells * width).astype(jnp.bfloat16)]
    pallas_call x0 -> x2, Pallas kernels: none -> 20.3 us  [the longest x1 12.7 us: local(): pl.pallas_call(functools.partial(add_kernel, nseg, cells, nnz_a, per), ou...]
    all_to_all x3 -> x2, waiting for transfers between devices: 156 us -> 138 us  [the longest x1 138 us: local(): lax.all_to_all(buffer, 'cell', 0, 0, tiled=True)]
    dot_general x2 -> x0, matrix products: 16.9 us -> none  [the longest x1 14.8 us: local(): jnp.einsum('csbm,cskbn->cskmn', got_p, got_products, preferred_element_ty...]
    reduce_sum x2 -> x0, other arithmetic: 15.3 us -> none  [the longest x1 15.1 us: local(): full_terms.reshape(cells, capacity, nnz_a, nnz_p, width, lanes).sum(3)]
    convert_element_type x2 -> x0, other arithmetic: 10.4 us -> none  [the longest x1 10.3 us: local(): summed.reshape(coarse_here, 3, 3, width, cells * width).astype(jnp.bfloat16)]
  transfers between devices with their start and end apart: 7 -> 6, of which waited for: 5 -> 2; matrix products, arithmetic and copies ran while one was open for 5% -> 1% of each run, Pallas kernels for 0% -> 0%
where the time goes in v1:
time: 198 us; the launch traced here: 196 us
  waiting for transfers between devices  139 us (70%)
  starting transfers between devices  32.7 us (17%)
  Pallas kernels  20.3 us (10%)
  local copies, waits for them, and re-layouts  2.44 us (1%)
    all_to_all x1, waiting for transfers between devices, local(): lax.all_to_all(buffer, 'cell', 0, 0, tiled=True)  138 us
    pallas_call x1, Pallas kernels, local(): pl.pallas_call(functools.partial(add_kernel, nseg, cells, nnz_a, per), ou...  12.7 us
    ppermute x4, starting transfers between devices, shifted(): return (lax.ppermute(value, axis, up), lax.ppermute(value, axis, down))  12.3 us
    all_to_all x1, starting transfers between devices, local(): lax.all_to_all(jnp.broadcast_to(meta[None], (cells, rows * 8)), 'cell', 0...  11.1 us
    all_to_all x1, starting transfers between devices, local(): lax.all_to_all(buffer, 'cell', 0, 0, tiled=True)  9.26 us
    pallas_call x1, Pallas kernels, local(): pl.pallas_call(functools.partial(send_kernel, rows, nnz_a), out_shape=jax...  7.61 us
  transfers between devices with their start and end apart: 6, of which 2 were waited for; matrix products, arithmetic and copies ran while one was open for 1% of the time, Pallas kernels for 0%

profile of v1, /device:TPU:9, one launch (start us, length us, event | category | flops | bytes accessed | tf_op | source)
XLA Modules:
  0.0 195.7 jit_solution(9876955880792975238)
XLA Ops:
  0.0 3.7 %collective-permute-start.2 = (bf16[16,64,128]{2,1,0:T(8,128)(2,1)}, bf16[16,64,128]{2,1,0:T(8,128)(2,1)S(1)}, u32[]{:S(2)}, u32[]{:S(2)}) collective-permute-start(bf16[16,64,128]{2,1,0:T(8,128)(2,1)} %pm.1), channel_id=1, source_target_pairs={{0,32},{32,64},{64,96},{96,128},{128,160},{160,192},{192,224},{1,3... | collective-permute-start | bytes 786440 | tf_op jit(solution)/shard_map/ppermute | solution.py:18
  3.7 1.9 collective-permute-start.3
  5.6 0.7 fusion.8
  6.3 0.7 pad_add_fusion.1
  7.0 0.1 copy.12
  7.1 0.1 broadcast_in_dim.44.meta
  7.2 0.6 broadcast_in_dim.45
  7.8 11.1 %all-to-all-start = ((s32[32,1,128]{2,1,0:T(1,128)}), s32[32,1,128]{2,1,0:T(1,128)S(1)}, u32[]{:S(2)}, u32[]{:S(2)}) async-start(s32[32,1,128]{2,1,0:T(1,128)} %broadcast_in_dim.45), calls=%async_computation | async-start | bytes 32768 | tf_op jit(solution)/shard_map/all_to_all | solution.py:150
  19.0 0.0 collective-permute-done.2.pb
  19.0 0.0 copy-start
  19.0 0.0 collective-permute-done.3.pa
  19.0 0.7 copy-done
  19.7 0.7 copy-done.1
  20.4 7.6 %send.1 = bf16[32,128,768]{2,1,0:T(8,128)(2,1)} custom-call(s32[128]{0:T(128)} %copy-done.2, bf16[16,64,384]{2,1,0:T(8,128)(2,1)} %a_ref.1, bf16[16,64,128]{2,1,0:T(8,128)(2,1)} %copy-done, bf16[16,64,128]{2,1,0:T(8,128)(2,1)} %pm.1, bf16[16,64,128]{2,1,0:T(8,128)(2,1)} %copy-done.1), custom_call_target="tpu_custom_call" | custom-call | tf_op jit(solution)/shard_map/send/pallas_call | solution.py:167
  28.0 9.3 %all-to-all-start.1 = ((bf16[32,128,768]{2,1,0:T(8,128)(2,1)}), bf16[32,128,768]{2,1,0:T(8,128)(2,1)}, u32[]{:S(2)}, u32[]{:S(2)}) async-start(bf16[32,128,768]{2,1,0:T(8,128)(2,1)} %send.1), calls=%async_computation.1 | async-start | bytes 12582912 | tf_op jit(solution)/shard_map/all_to_all | solution.py:182
  37.3 1.9 collective-permute-start.1
  39.2 4.8 %collective-permute-start = (s32[32,128]{1,0:T(8,128)S(1)}, s32[32,128]{1,0:T(8,128)S(1)}, u32[]{:S(2)}, u32[]{:S(2)}) collective-permute-start(s32[32,128]{1,0:T(8,128)S(1)} %bitcast.15), channel_id=1, source_target_pairs={{0,32},{32,64},{64,96},{96,128},{128,160},{160,192},{192,224},{1,3... | collective-permute-start | bytes 49160 | tf_op jit(solution)/shard_map/ppermute | solution.py:18
  44.0 0.1 copy.13
  44.1 0.1 select_reduce_fusion.1
  44.3 0.1 copy.14
  44.3 0.1 reshape.105.slots
  44.5 0.4 collective-permute-done
  44.9 138.2 %all-to-all-done.1 = bf16[32,128,768]{2,1,0:T(8,128)(2,1)} async-done(((bf16[32,128,768]{2,1,0:T(8,128)(2,1)}), bf16[32,128,768]{2,1,0:T(8,128)(2,1)}, u32[]{:S(2)}, u32[]{:S(2)}) %all-to-all-start.1) | async-done | bytes 6291488 | tf_op jit(solution)/shard_map/all_to_all | solution.py:182
  183.1 12.7 %add.75 = bf16[18,64,2048]{2,1,0:T(8,128)(2,1)} custom-call(s32[12288]{0:T(1024)S(1)} %bitcast.13, s32[64]{0:T(128)S(1)} %reshape.105.slots, bf16[64,64,768]{2,1,0:T(8,128)(2,1)} %bitcast.8.got), custom_call_target="tpu_custom_call" | custom-call | tf_op jit(solution)/shard_map/add/pallas_call | solution.py:184
  (10 shorter events, 0.0 us)
Async XLA Ops:
  0.0 19.0 %collective-permute-start.2 = (bf16[16,64,128]{2,1,0:T(8,128)(2,1)}, bf16[16,64,128]{2,1,0:T(8,128)(2,1)S(1)}, u32[]{:S(2)}, u32[]{:S(2)}) collective-permute-start(bf16[16,64,128]{2,1,0:T(8,128)(2,1)} %pm.1), channel_id=1, source_target_pairs={{0,32},{32,64},{64,96},{96,128},{128,160},{160,192},{192,224},{1,3... | collective-permute-start | bytes 786440 | tf_op jit(solution)/shard_map/ppermute | solution.py:18
  3.7 15.3 %collective-permute-start.3 = (bf16[16,64,128]{2,1,0:T(8,128)(2,1)}, bf16[16,64,128]{2,1,0:T(8,128)(2,1)S(1)}, u32[]{:S(2)}, u32[]{:S(2)}) collective-permute-start(bf16[16,64,128]{2,1,0:T(8,128)(2,1)} %pm.1), channel_id=1, source_target_pairs={{32,0},{64,32},{96,64},{128,96},{160,128},{192,160},{224,192},{33,... | collective-permute-start | bytes 786440 | tf_op jit(solution)/shard_map/ppermute | solution.py:18
  7.2 11.8 %copy-start.2 = (s32[128]{0:T(128)}, s32[128]{0:T(128)S(1)}, u32[]{:S(2)}) copy-start(s32[128]{0:T(128)S(1)} %broadcast_in_dim.44.meta) | copy-start | bytes 1540
  7.8 20.2 %all-to-all-start = ((s32[32,1,128]{2,1,0:T(1,128)}), s32[32,1,128]{2,1,0:T(1,128)S(1)}, u32[]{:S(2)}, u32[]{:S(2)}) async-start(s32[32,1,128]{2,1,0:T(1,128)} %broadcast_in_dim.45), calls=%async_computation | async-start | bytes 32768 | tf_op jit(solution)/shard_map/all_to_all | solution.py:150
  19.0 0.7 copy-start
  19.7 0.7 copy-start.1
  28.0 155.1 %all-to-all-start.1 = ((bf16[32,128,768]{2,1,0:T(8,128)(2,1)}), bf16[32,128,768]{2,1,0:T(8,128)(2,1)}, u32[]{:S(2)}, u32[]{:S(2)}) async-start(bf16[32,128,768]{2,1,0:T(8,128)(2,1)} %send.1), calls=%async_computation.1 | async-start | bytes 12582912 | tf_op jit(solution)/shard_map/all_to_all | solution.py:182
  37.3 7.2 %collective-permute-start.1 = (s32[32,128]{1,0:T(8,128)S(1)}, s32[32,128]{1,0:T(8,128)S(1)}, u32[]{:S(2)}, u32[]{:S(2)}) collective-permute-start(s32[32,128]{1,0:T(8,128)S(1)} %bitcast.14), channel_id=1, source_target_pairs={{32,0},{64,32},{96,64},{128,96},{160,128},{192,160},{224,192},{33,... | collective-permute-start | bytes 49160 | tf_op jit(solution)/shard_map/ppermute | solution.py:18
  39.2 5.7 %collective-permute-start = (s32[32,128]{1,0:T(8,128)S(1)}, s32[32,128]{1,0:T(8,128)S(1)}, u32[]{:S(2)}, u32[]{:S(2)}) collective-permute-start(s32[32,128]{1,0:T(8,128)S(1)} %bitcast.15), channel_id=1, source_target_pairs={{0,32},{32,64},{64,96},{96,128},{128,160},{160,192},{192,224},{1,3... | collective-permute-start | bytes 49160 | tf_op jit(solution)/shard_map/ppermute | solution.py:18

commit v2 on v0

v2 whole, which is shorter than its diff:
```python
import functools

import jax
import jax.numpy as jnp
from jax import lax
from jax.experimental import pallas as pl
from jax.experimental.pallas import tpu as pltpu
from jax.sharding import Mesh
from jax.sharding import PartitionSpec as P


AGG = 8
BS = 64
ANY = pl.BlockSpec(memory_space=pl.ANY)
SMEM = pl.BlockSpec(memory_space=pltpu.SMEM)


def shifted(value):
    n = lax.axis_size("frame")
    before = lax.ppermute(value, "frame", [(i, i + 1) for i in range(n - 1)])
    after = lax.ppermute(value, "frame", [(i + 1, i) for i in range(n - 1)])
    return before, after


def turned(up, down):
    n = lax.axis_size("z")
    up = lax.ppermute(up, "z", [(i, (i + 1) % n) for i in range(n)])
    if down is None:
        return (up,)
    down = lax.ppermute(down, "z", [((i + 1) % n, i) for i in range(n)])
    return up, down


def term_kernel(rows, nnz_a, nz, ny, offsets, pieces, first, meta, here, *refs):
    count = len(offsets)
    npieces = len(pieces)
    a_refs, p_refs = refs[:npieces], refs[npieces : npieces + count]
    before, after, out, abuf, pall, apbuf, obuf, placed, listed, sems = refs[npieces + count :]
    copies = []

    def fetch(src, dst):
        copy = pltpu.make_async_copy(src, dst, sems.at[len(copies)])
        copy.start()
        copies.append(copy)

    for (s, start, size), a_ref in zip(pieces, a_refs):
        fetch(a_ref, abuf.at[s, pl.ds(start, size)])
    for s, p_ref in enumerate(p_refs[:count]):
        fetch(p_ref, pall.at[s, pl.ds(rows, rows)])
        fetch(before.at[pl.ds((first + s) * rows, rows)], pall.at[s, pl.ds(0, rows)])
        fetch(after.at[pl.ds((first + s) * rows, rows)], pall.at[s, pl.ds(2 * rows, rows)])
    z, y = here[0], here[1]
    bases, active = [], []
    for s, offset in enumerate(offsets):
        base = (lax.rem(z + offset + nz, nz) * ny + y) * 128
        bases.append(base)
        for i in range(ny):
            placed[s * ny + i] = 0
        listed[s * (rows + 1)] = 0

        def look(r, n, s=s, base=base):
            z0 = meta[base + r * 8 + 6] // ny
            z1 = meta[base + r * 8 + 7] // ny
            listed[s * (rows + 1) + n] = r
            return n + jnp.where((z0 == z) | (z1 == z), 1, 0)

        active.append(lax.fori_loop(0, rows, look, 0))
    for copy in copies:
        copy.wait()
    zero = jnp.zeros((BS, 2 * BS), jnp.bfloat16)
    trash = ny * 2 * count

    def row(i, _):
        picked = []
        for s in range(count):
            live = i < active[s]
            r = listed[s * (rows + 1) + jnp.where(live, i, 0)]
            base = bases[s] + r * 8
            picked.append((live, r, base))
            for m in range(nnz_a // 2):
                f0 = meta[base + 2 * m] & 63
                f1 = meta[base + 2 * m + 1] & 63
                rhs = jnp.concatenate(
                    [
                        jnp.concatenate([pall[s, f0], zero], axis=1),
                        jnp.concatenate([zero, pall[s, f1]], axis=1),
                    ],
                    axis=0,
                )
                ap = jnp.dot(
                    abuf[s, r, :, 2 * BS * m : 2 * BS * (m + 1)],
                    rhs,
                    preferred_element_type=jnp.float32,
                )
                apbuf[s, :, 4 * BS * m : 4 * BS * (m + 1)] = ap.astype(jnp.bfloat16)
        for s in range(count):
            live, r, base = picked[s]
            t = lax.dot_general(
                pall[s, rows + r],
                apbuf[s],
                (((0,), (0,)), ((), ())),
                preferred_element_type=jnp.float32,
            ).astype(jnp.bfloat16)
            for p in range(2):
                c = meta[base + 6 + p] - z * ny
                fits = live & (c >= 0) & (c < ny)
                c = jnp.where(fits, c, 0)
                place = placed[s * ny + c]
                placed[s * ny + c] = place + jnp.where(fits, 1, 0)
                slot = jnp.where(fits, c * (2 * count) + 2 * s + place, trash)
                obuf[slot] = t[p * BS : (p + 1) * BS]
        return 0

    most = active[0]
    for n in active[1:]:
        most = jnp.maximum(most, n)
    lax.fori_loop(0, most, row, 0)
    copy = pltpu.make_async_copy(obuf.at[pl.ds(0, trash)], out, sems.at[0])
    copy.start()
    copy.wait()


def add_kernel(nseg, nz, ny, nnz_a, offsets, meta, slots, here, *refs):
    chunks = len(offsets)
    got, out, bufs = refs[:chunks], refs[chunks], refs[chunks + 1 : 2 * chunks + 1]
    acc, stage, insems, sems = refs[2 * chunks + 1 :]
    cells = nz * ny
    for i in range(chunks):
        pltpu.make_async_copy(got[i], bufs[i], insems.at[i]).start()

    def clear(j, _):
        acc[pl.ds(j * 4, 4)] = jnp.zeros((4,) + acc.shape[1:], jnp.float32)
        return 0

    lax.fori_loop(0, acc.shape[0] // 4, clear, 0)
    low = lax.broadcasted_iota(jnp.int32, (BS, 2 * BS), 1) < BS
    z = here[0]
    for i in range(chunks):
        pltpu.make_async_copy(got[i], bufs[i], insems.at[i]).wait()
        for s, offset in enumerate(offsets[i]):
            zs = lax.rem(z + offset + nz, nz)

            def slot(j, _, i=i, s=s, zs=zs):
                y = j // 2
                c = zs * ny + y
                e = slots[2 * c + (j & 1)]

                @pl.when(e >= 0)
                def _():
                    base = cells * 128 + c * 128 + (e // 2) * 8
                    for k in range(nnz_a):
                        w = meta[base + k]
                        far = w & 63
                        seg = w >> 6
                        src = (far >> 4) * (cells * 128) + c * 128 + (far & 15) * 8 + 6
                        i0 = seg * cells + meta[src]
                        i1 = seg * cells + meta[src + 1]
                        x = bufs[i][y, 2 * s + (j & 1), :, 2 * BS * k : 2 * BS * (k + 1)]
                        x = x.astype(jnp.float32)
                        new0 = acc[i0] + jnp.where(low, x, 0.0)
                        new1 = acc[i1] + jnp.where(low, 0.0, x)
                        acc[i0] = new0
                        acc[i1] = new1

                return 0

            lax.fori_loop(0, 2 * ny, slot, 0)

    def put(seg, _):
        for h in range(cells // 2):
            a = acc[seg * cells + 2 * h]
            b = acc[seg * cells + 2 * h + 1]
            v = jnp.where(low, a, b) + pltpu.roll(jnp.where(low, b, a), BS, 1)
            stage[seg, :, 2 * BS * h : 2 * BS * (h + 1)] = v.astype(jnp.bfloat16)
        pltpu.make_async_copy(stage.at[seg], out.at[seg], sems.at[seg]).start()
        return 0

    lax.fori_loop(0, nseg, put, 0)

    def finish(seg, _):
        pltpu.make_async_copy(stage.at[seg], out.at[seg], sems.at[seg]).wait()
        return 0

    lax.fori_loop(0, nseg, finish, 0)


def last_kernel(nz, ny, nnz_a, offset, meta, slots, here, part, got, out, buf, stage, sems):
    cells = nz * ny
    loads = [
        pltpu.make_async_copy(part, stage, sems.at[0]),
        pltpu.make_async_copy(got, buf, sems.at[1]),
    ]
    for copy in loads:
        copy.start()
    for copy in loads:
        copy.wait()
    upper = lax.broadcasted_iota(jnp.int32, (BS, 2 * BS), 1) // BS
    zs = lax.rem(here[0] + offset + nz, nz)

    def slot(j, _):
        y = j // 2
        c = zs * ny + y
        e = slots[2 * c + (j & 1)]

        @pl.when(e >= 0)
        def _():
            base = cells * 128 + c * 128 + (e // 2) * 8
            for k in range(nnz_a):
                w = meta[base + k]
                far = w & 63
                seg = w >> 6
                src = (far >> 4) * (cells * 128) + c * 128 + (far & 15) * 8 + 6
                x = buf[y, j & 1, :, 2 * BS * k : 2 * BS * (k + 1)].astype(jnp.float32)
                turned_x = pltpu.roll(x, BS, 1)
                for q in range(2):
                    cell = meta[src + q]
                    side = cell & 1
                    lanes = pl.ds(pl.multiple_of((cell >> 1) * (2 * BS), 2 * BS), 2 * BS)
                    v = jnp.where(upper == side, jnp.where(side == q, x, turned_x), 0.0)
                    old = stage[seg, :, lanes].astype(jnp.float32)
                    stage[seg, :, lanes] = (old + v).astype(jnp.bfloat16)

        return 0

    lax.fori_loop(0, 2 * ny, slot, 0)
    copy = pltpu.make_async_copy(stage, out, sems.at[2])
    copy.start()
    copy.wait()


def local(a_blocks, a_cols, p_blocks, p_cells):
    rows = a_blocks.shape[0]
    nnz_a = a_cols.shape[1]
    nz, ny = lax.axis_size("z"), lax.axis_size("y")
    cells = nz * ny
    frame, z, y = lax.axis_index("frame"), lax.axis_index("z"), lax.axis_index("y")
    coarse_here = rows // AGG
    nseg = coarse_here * 9
    half = nz // 2
    mid = rows // 2
    wide = 2 * nnz_a * BS

    p_ring, a_ring = [(p_blocks, p_blocks)], [(a_blocks, a_blocks)]
    for d in range(1, half + 1):
        up, down = p_ring[-1]
        p_ring.append(turned(up, None if d == half else down))
        up, down = a_ring[-1]
        if d == half:
            up, down = up[:mid], down[mid:]
        a_ring.append(turned(up, down))

    where_u = lax.div(a_cols, jnp.int32(rows * cells)) - frame + 1
    where_r = a_cols & (rows - 1)
    agg = jnp.arange(rows, dtype=jnp.int32)[:, None] // AGG
    seg = agg * 9 + where_u * 3 + where_r // AGG - agg + 1
    meta = jnp.concatenate([where_u * rows + where_r + 64 * seg, p_cells], axis=1).reshape(rows * 8)
    everyone = lax.all_to_all(
        jnp.broadcast_to(meta[None], (cells, rows * 8)), ("z", "y"), 0, 0, tiled=True
    )
    mb, ma = shifted(everyone)
    three = jnp.stack([mb, everyone, ma]).reshape(-1)
    flat = everyone.reshape(-1)
    named = everyone.reshape(cells, rows, 8)[:, :, 6:].reshape(cells, 2 * rows)
    entry = jnp.arange(2 * rows, dtype=jnp.int32)[None]
    hit = named == z * ny + y
    first = jnp.min(jnp.where(hit, entry, 2 * rows), axis=1)
    last = jnp.max(jnp.where(hit, entry, -1), axis=1)
    slots = jnp.stack(
        [jnp.where(first < 2 * rows, first, -1), jnp.where(last > first, last, -1)], axis=1
    ).reshape(2 * cells)
    here = jnp.stack([z, y]).astype(jnp.int32)

    whole = (0, rows)
    whole = (0, rows)
    three_rings = zip((p_blocks,) + p_ring[1], (a_blocks,) + a_ring[1])
    p_list, a_list = zip(*three_rings)
    groups = [((0, -1, 1), tuple((i, *whole) for i in range(3)), a_list, p_list, 0, 0)]
    for d in range(2, half):
        groups.append(((-d, d), ((0, *whole), (1, *whole)), a_ring[d], p_ring[d], d - 1, 0))
    groups.append(((half,), ((0, 0, mid), (0, mid, mid)), a_ring[half], p_ring[half], 2, 2))
    batches = [
        (p_blocks,) + p_ring[1],
        p_ring[2],
        p_ring[3] + p_ring[4],
    ]
    near = {}
    got = []
    for i, (offsets, pieces, a_list, p_list, batch, start) in enumerate(groups):
        if batch not in near:
            parts = batches[batch]
            if i == 2:
                *parts, sent = lax.optimization_barrier((*parts, sent))
            near[batch] = shifted(jnp.concatenate(parts, axis=0))
        if i > 0:
            if i > 1:
                sent, got[-1] = lax.optimization_barrier((sent, got[-1]))
            got.append(lax.all_to_all(sent, "y", 0, 0, tiled=True))
        pb, pa = near[batch]
        count = len(offsets)
        sent = pl.pallas_call(
            functools.partial(term_kernel, rows, nnz_a, nz, ny, offsets, pieces, start),
            out_shape=jax.ShapeDtypeStruct((ny * 2 * count, BS, wide), jnp.bfloat16),
            in_specs=[SMEM, SMEM] + [ANY] * (len(a_list) + len(p_list) + 2),
            out_specs=ANY,
            scratch_shapes=[
                pltpu.VMEM((count, rows, BS, nnz_a * BS), jnp.bfloat16),
                pltpu.VMEM((count, 3 * rows, BS, 2 * BS), jnp.bfloat16),
                pltpu.VMEM((count, BS, wide), jnp.bfloat16),
                pltpu.VMEM((ny * 2 * count + 1, BS, wide), jnp.bfloat16),
                pltpu.SMEM((count * ny,), jnp.int32),
                pltpu.SMEM((count * (rows + 1),), jnp.int32),
                pltpu.SemaphoreType.DMA((len(pieces) + 3 * count,)),
            ],
            compiler_params=pltpu.CompilerParams(vmem_limit_bytes=24 << 20),
            name="terms",
        )(flat, here, *a_list, *p_list, pb, pa)
        sent = sent.reshape(ny, 2 * count, BS, wide)
    sent, got[-1] = lax.optimization_barrier((sent, got[-1]))
    got.append(lax.all_to_all(sent, "y", 0, 0, tiled=True))
    offsets = [g[0] for g in groups]
    result = jax.ShapeDtypeStruct((nseg, BS, cells * BS), jnp.bfloat16)
    early = got[:-1]
    part = pl.pallas_call(
        functools.partial(add_kernel, nseg, nz, ny, nnz_a, offsets[:-1]),
        out_shape=result,
        in_specs=[SMEM, SMEM, SMEM] + [ANY] * len(early),
        out_specs=ANY,
        scratch_shapes=[pltpu.VMEM(g.shape, g.dtype) for g in early]
        + [
            pltpu.VMEM((nseg * cells, BS, 2 * BS), jnp.float32),
            pltpu.VMEM(result.shape, result.dtype),
            pltpu.SemaphoreType.DMA((len(early),)),
            pltpu.SemaphoreType.DMA((nseg,)),
        ],
        compiler_params=pltpu.CompilerParams(vmem_limit_bytes=60 << 20),
        name="add",
    )(three, slots, here, *early)
    out = pl.pallas_call(
        functools.partial(last_kernel, nz, ny, nnz_a, half),
        out_shape=result,
        in_specs=[SMEM, SMEM, SMEM, ANY, ANY],
        out_specs=ANY,
        scratch_shapes=[
            pltpu.VMEM(got[-1].shape, jnp.bfloat16),
            pltpu.VMEM(result.shape, result.dtype),
            pltpu.SemaphoreType.DMA((3,)),
        ],
        compiler_params=pltpu.CompilerParams(vmem_limit_bytes=60 << 20),
        name="finish",
    )(three, slots, here, part, got[-1])
    return out.reshape(coarse_here, 3, 3, BS, cells * BS)


def solution(mesh):
    frames = mesh.shape["frame"]
    grid = Mesh(mesh.devices.reshape(frames, 8, -1), ("frame", "z", "y"))
    dim = ("frame", "z", "y")

    return jax.shard_map(
        local,
        mesh=grid,
        in_specs=(P(dim, None, None), P(dim, None), P(dim, None, None), P(dim, None)),
        out_specs=P(dim, None, None, None, None),
        check_vma=False,
    )
```

time: 478 us -> 192 us (0.40)
  the two profiles are of different devices: /device:TPU:9 before, /device:TPU:1 now
where the time goes in v2:
time: 192 us; the launch traced here: 191 us
  starting transfers between devices  78 us (41%)
  waiting for transfers between devices  59 us (31%)
  Pallas kernels  41 us (21%)
  local copies, waits for them, and re-layouts  9.9 us (5%)
  other arithmetic  2.23 us (1%)
    ppermute x8, waiting for transfers between devices, turned(): up = lax.ppermute(up, 'z', [(i, (i + 1) % n) for i in range(n)])  32.5 us
    pallas_call x4, Pallas kernels, local(): pl.pallas_call(functools.partial(term_kernel, rows, nnz_a, nz, ny, offset...  20.4 us
    ppermute x4, starting transfers between devices, shifted(): after = lax.ppermute(value, 'frame', [(i + 1, i) for i in range(n - 1)])  18 us
    all_to_all x4, starting transfers between devices, local(): got.append(lax.all_to_all(sent, 'y', 0, 0, tiled=True))  16.9 us
    ppermute x7, starting transfers between devices, turned(): down = lax.ppermute(down, 'z', [((i + 1) % n, i) for i in range(n)])  16.7 us
    ppermute x4, starting transfers between devices, shifted(): before = lax.ppermute(value, 'frame', [(i, i + 1) for i in range(n - 1)])  13 us
    pallas_call x1, Pallas kernels, local(): pl.pallas_call(functools.partial(add_kernel, nseg, nz, ny, nnz_a, offsets...  12.7 us
    ppermute x7, waiting for transfers between devices, turned(): down = lax.ppermute(down, 'z', [((i + 1) % n, i) for i in range(n)])  10.2 us
  transfers between devices with their start and end apart: 28, of which 10 were waited for; matrix products, arithmetic and copies ran while one was open for 4% of the time, Pallas kernels for 14%

profile of v2, /device:TPU:1, one launch (start us, length us, event | category | flops | bytes accessed | tf_op | source)
XLA Modules:
  0.0 190.7 jit_solution(14772947682338819616)
XLA Ops:
  2.5 3.9 %collective-permute-start.5 = (bf16[16,64,128]{2,1,0:T(8,128)(2,1)}, bf16[16,64,128]{2,1,0:T(8,128)(2,1)S(1)}, u32[]{:S(2)}, u32[]{:S(2)}) collective-permute-start(bf16[16,64,128]{2,1,0:T(8,128)(2,1)} %refs_3_.1), channel_id=1, source_target_pairs={{4,0},{8,4},{12,8},{16,12},{20,16},{24,20},{28,24},{0,28},{5,1},{9... | collective-permute-start | bytes 786440 | tf_op jit(solution)/shard_map/ppermute | solution.py:30
  14.1 4.0 %collective-permute-start.16 = (bf16[48,64,128]{2,1,0:T(8,128)(2,1)}, bf16[48,64,128]{2,1,0:T(8,128)(2,1)S(1)}, u32[]{:S(2)}, u32[]{:S(2)}) collective-permute-start(bf16[48,64,128]{2,1,0:T(8,128)(2,1)} %constant_dynamic-update-slice_fusion.2), channel_id=1, source_target_pairs={{32,0},{64,32},{96,64},{128,96},{160,128},{192,160},{224,192},{33,... | collective-permute-start | bytes 2359304 | tf_op jit(solution)/shard_map/ppermute | solution.py:21
  23.3 8.6 %all-to-all-start = ((s32[32,1,128]{2,1,0:T(1,128)}), s32[32,1,128]{2,1,0:T(1,128)S(1)}, u32[]{:S(2)}, u32[]{:S(2)}) async-start(s32[32,1,128]{2,1,0:T(1,128)} %broadcast_in_dim.45), calls=%async_computation | async-start | bytes 32768 | tf_op jit(solution)/shard_map/all_to_all | solution.py:257
  32.0 8.5 %all-to-all-done = s32[32,1,128]{2,1,0:T(1,128)S(1)} async-done(((s32[32,1,128]{2,1,0:T(1,128)}), s32[32,1,128]{2,1,0:T(1,128)S(1)}, u32[]{:S(2)}, u32[]{:S(2)}) %all-to-all-start) | async-done | bytes 16416 | tf_op jit(solution)/shard_map/all_to_all | solution.py:257
  42.6 6.0 %terms.5 = bf16[24,64,768]{2,1,0:T(8,128)(2,1)} custom-call(s32[4096]{0:T(1024)S(1)} %bitcast.19, s32[2]{0:T(128)S(1)} %pad_add_fusion.3.here, bf16[16,64,384]{2,1,0:T(8,128)(2,1)S(1)} %copy-done.5, bf16[16,64,384]{2,1,0:T(8,128)(2,1)S(1)} %collective-permute-done.9.refs_1_, bf16[16,64,384]{2,1,0:T(8,128)(2,1)S(1)} %collective-permute-done.11.refs_2_, ...), custom_call_target="tpu_custom_call" | custom-call | tf_op jit(solution)/shard_map/terms/pallas_call | solution.py:300
  48.6 4.5 %all-to-all-start.1 = ((bf16[4,6,64,768]{3,2,1,0:T(8,128)(2,1)}), bf16[4,6,64,768]{3,2,1,0:T(8,128)(2,1)}, u32[]{:S(2)}, u32[]{:S(2)}) async-start(bf16[4,6,64,768]{3,2,1,0:T(8,128)(2,1)} %bitcast.12), calls=%async_computation.1 | async-start | bytes 4718592 | tf_op jit(solution)/shard_map/all_to_all | solution.py:297
  55.9 4.8 %collective-permute-done.3.refs_2_ = bf16[16,64,128]{2,1,0:T(8,128)(2,1)S(1)} collective-permute-done((bf16[16,64,128]{2,1,0:T(8,128)(2,1)S(1)}, bf16[16,64,128]{2,1,0:T(8,128)(2,1)S(1)}, u32[]{:S(2)}, u32[]{:S(2)}) %collective-permute-start.3) | collective-permute-done | bytes 262176 | tf_op jit(solution)/shard_map/ppermute | solution.py:27
  63.6 4.9 %collective-permute-start.14 = (bf16[32,64,128]{2,1,0:T(8,128)(2,1)S(1)}, bf16[32,64,128]{2,1,0:T(8,128)(2,1)S(1)}, u32[]{:S(2)}, u32[]{:S(2)}) collective-permute-start(bf16[32,64,128]{2,1,0:T(8,128)(2,1)S(1)} %constant_dynamic-update-slice_fusion), channel_id=1, source_target_pairs={{32,0},{64,32},{96,64},{128,96},{160,128},{192,160},{224,192},{33,... | collective-permute-start | bytes 1572872 | tf_op jit(solution)/shard_map/ppermute | solution.py:21
  71.6 12.9 %collective-permute-done.4.refs_2_ = bf16[16,64,128]{2,1,0:T(8,128)(2,1)S(1)} collective-permute-done((bf16[16,64,128]{2,1,0:T(8,128)(2,1)S(1)}, bf16[16,64,128]{2,1,0:T(8,128)(2,1)S(1)}, u32[]{:S(2)}, u32[]{:S(2)}) %collective-permute-start.4) | collective-permute-done | bytes 262176 | tf_op jit(solution)/shard_map/ppermute | solution.py:27
  85.9 5.3 %terms.4 = bf16[16,64,768]{2,1,0:T(8,128)(2,1)} custom-call(s32[4096]{0:T(1024)S(1)} %bitcast.20, s32[2]{0:T(128)S(1)} %pad_add_fusion.3.here, bf16[16,64,384]{2,1,0:T(8,128)(2,1)} %collective-permute-done.10.refs_0_, bf16[16,64,384]{2,1,0:T(8,128)(2,1)S(1)} %collective-permute-done.12.refs_1_, bf16[16,64,128]{2,1,0:T(8,128)(2,1)S(1)} %collective-permute-done.3.refs_2_, ...), custom_call_target="tpu_custom_call" | custom-call | tf_op jit(solution)/shard_map/terms/pallas_call | solution.py:300
  91.2 4.4 %all-to-all-start.2 = ((bf16[4,4,64,768]{3,2,1,0:T(8,128)(2,1)}), bf16[4,4,64,768]{3,2,1,0:T(8,128)(2,1)}, u32[]{:S(2)}, u32[]{:S(2)}) async-start(bf16[4,4,64,768]{3,2,1,0:T(8,128)(2,1)} %bitcast.11), calls=%async_computation.2 | async-start | bytes 3145728 | tf_op jit(solution)/shard_map/all_to_all | solution.py:297
  96.0 6.7 %collective-permute-start.20 = (bf16[48,64,128]{2,1,0:T(8,128)(2,1)S(1)}, bf16[48,64,128]{2,1,0:T(8,128)(2,1)S(1)}, u32[]{:S(2)}, u32[]{:S(2)}) collective-permute-start(bf16[48,64,128]{2,1,0:T(8,128)(2,1)S(1)} %constant_dynamic-update-slice_fusion.5), channel_id=1, source_target_pairs={{32,0},{64,32},{96,64},{128,96},{160,128},{192,160},{224,192},{33,... | collective-permute-start | bytes 2359304 | tf_op jit(solution)/shard_map/ppermute | solution.py:21
  102.7 3.9 %collective-permute-start.19 = (bf16[48,64,128]{2,1,0:T(8,128)(2,1)S(1)}, bf16[48,64,128]{2,1,0:T(8,128)(2,1)S(1)}, u32[]{:S(2)}, u32[]{:S(2)}) collective-permute-start(bf16[48,64,128]{2,1,0:T(8,128)(2,1)S(1)} %constant_dynamic-update-slice_fusion.5), channel_id=1, source_target_pairs={{0,32},{32,64},{64,96},{96,128},{128,160},{160,192},{192,224},{1,3... | collective-permute-start | bytes 2359304 | tf_op jit(solution)/shard_map/ppermute | solution.py:20
  108.8 3.5 %collective-permute-done.17.refs_0_ = bf16[16,64,384]{2,1,0:T(8,128)(2,1)S(1)} collective-permute-done((bf16[16,64,384]{2,1,0:T(8,128)(2,1)}, bf16[16,64,384]{2,1,0:T(8,128)(2,1)S(1)}, u32[]{:S(2)}, u32[]{:S(2)}) %collective-permute-start.17) | collective-permute-done | bytes 786464 | tf_op jit(solution)/shard_map/ppermute | solution.py:27
  115.5 10.1 %collective-permute-done.18.refs_1_ = bf16[16,64,384]{2,1,0:T(8,128)(2,1)S(1)} collective-permute-done((bf16[16,64,384]{2,1,0:T(8,128)(2,1)}, bf16[16,64,384]{2,1,0:T(8,128)(2,1)S(1)}, u32[]{:S(2)}, u32[]{:S(2)}) %collective-permute-start.18) | collective-permute-done | bytes 786464 | tf_op jit(solution)/shard_map/ppermute | solution.py:30
  127.5 4.9 %terms.6 = bf16[16,64,768]{2,1,0:T(8,128)(2,1)} custom-call(s32[4096]{0:T(1024)S(1)} %bitcast.21, s32[2]{0:T(128)S(1)} %pad_add_fusion.3.here, bf16[16,64,384]{2,1,0:T(8,128)(2,1)S(1)} %collective-permute-done.17.refs_0_, bf16[16,64,384]{2,1,0:T(8,128)(2,1)S(1)} %collective-permute-done.18.refs_1_, bf16[16,64,128]{2,1,0:T(8,128)(2,1)S(1)} %copy-done.2, ...), custom_call_target="tpu_custom_call" | custom-call | tf_op jit(solution)/shard_map/terms/pallas_call | solution.py:300
  132.4 4.5 %all-to-all-start.3 = ((bf16[4,4,64,768]{3,2,1,0:T(8,128)(2,1)}), bf16[4,4,64,768]{3,2,1,0:T(8,128)(2,1)}, u32[]{:S(2)}, u32[]{:S(2)}) async-start(bf16[4,4,64,768]{3,2,1,0:T(8,128)(2,1)} %bitcast.13), calls=%async_computation.3 | async-start | bytes 3145728 | tf_op jit(solution)/shard_map/all_to_all | solution.py:297
  139.8 9.4 %collective-permute-done.21.refs_0_ = bf16[8,64,384]{2,1,0:T(8,128)(2,1)S(1)} collective-permute-done((bf16[8,64,384]{2,1,0:T(8,128)(2,1)S(1)}, bf16[8,64,384]{2,1,0:T(8,128)(2,1)S(1)}, u32[]{:S(2)}, u32[]{:S(2)}) %collective-permute-start.21) | collective-permute-done | bytes 393248 | tf_op jit(solution)/shard_map/ppermute | solution.py:27
  149.3 4.3 %terms.7 = bf16[8,64,768]{2,1,0:T(8,128)(2,1)} custom-call(s32[4096]{0:T(1024)S(1)} %bitcast.22, s32[2]{0:T(128)S(1)} %pad_add_fusion.3.here, bf16[8,64,384]{2,1,0:T(8,128)(2,1)S(1)} %collective-permute-done.21.refs_0_, bf16[8,64,384]{2,1,0:T(8,128)(2,1)S(1)} %collective-permute-done.22.refs_1_, bf16[16,64,128]{2,1,0:T(8,128)(2,1)S(1)} %collective-permute-done.8.refs_2_, ...), custom_call_target="tpu_custom_call" | custom-call | tf_op jit(solution)/shard_map/terms/pallas_call | solution.py:300
  153.5 4.7 %all-to-all-done.3.refs_2_ = bf16[4,4,64,768]{3,2,1,0:T(8,128)(2,1)} async-done(((bf16[4,4,64,768]{3,2,1,0:T(8,128)(2,1)}), bf16[4,4,64,768]{3,2,1,0:T(8,128)(2,1)}, u32[]{:S(2)}, u32[]{:S(2)}) %all-to-all-start.3) | async-done | bytes 1572896 | tf_op jit(solution)/shard_map/all_to_all | solution.py:297
  158.2 3.5 %all-to-all-start.4 = ((bf16[4,2,64,768]{3,2,1,0:T(8,128)(2,1)}), bf16[4,2,64,768]{3,2,1,0:T(8,128)(2,1)S(1)}, u32[]{:S(2)}, u32[]{:S(2)}) async-start(bf16[4,2,64,768]{3,2,1,0:T(8,128)(2,1)} %bitcast.14), calls=%async_computation.4 | async-start | bytes 1572864 | tf_op jit(solution)/shard_map/all_to_all | solution.py:319
  164.2 3.1 %collective-permute-start = (s32[32,128]{1,0:T(8,128)S(1)}, s32[32,128]{1,0:T(8,128)S(1)}, u32[]{:S(2)}, u32[]{:S(2)}) collective-permute-start(s32[32,128]{1,0:T(8,128)S(1)} %bitcast.24), channel_id=1, source_target_pairs={{0,32},{32,64},{64,96},{96,128},{128,160},{160,192},{192,224},{1,3... | collective-permute-start | bytes 49160 | tf_op jit(solution)/shard_map/ppermute | solution.py:20
  169.0 12.7 %add.81.part = bf16[18,64,2048]{2,1,0:T(8,128)(2,1)} custom-call(s32[12288]{0:T(1024)} %bitcast.26, s32[64]{0:T(128)} %reshape.117.slots, s32[2]{0:T(128)} %copy-done.7, bf16[4,6,64,768]{3,2,1,0:T(8,128)(2,1)} %all-to-all-done.1.refs_0_, bf16[4,4,64,768]{3,2,1,0:T(8,128)(2,1)} %all-to-all-done.2.refs_1_, bf16[4,4,64,768]{3,2,1,0:T(8,128)(2,1)} %all-to-all-done.3.refs_2_), custom_call_target="tpu_custom_call" | custom-call | tf_op jit(solution)/shard_map/add/pallas_call | solution.py:323
  182.7 7.9 %finish.1 = bf16[18,64,2048]{2,1,0:T(8,128)(2,1)} custom-call(s32[12288]{0:T(1024)} %bitcast.27, s32[64]{0:T(128)} %reshape.117.slots, s32[2]{0:T(128)} %copy-done.7, bf16[18,64,2048]{2,1,0:T(8,128)(2,1)} %add.81.part, bf16[4,2,64,768]{3,2,1,0:T(8,128)(2,1)} %copy-done.8), custom_call_target="tpu_custom_call" | custom-call | tf_op jit(solution)/shard_map/finish/pallas_call | solution.py:338
  (81 shorter events, 43.2 us)
Async XLA Ops:
  0.0 12.6 %collective-permute-start.2 = (bf16[16,64,128]{2,1,0:T(8,128)(2,1)}, bf16[16,64,128]{2,1,0:T(8,128)(2,1)S(1)}, u32[]{:S(2)}, u32[]{:S(2)}) collective-permute-start(bf16[16,64,128]{2,1,0:T(8,128)(2,1)} %refs_3_.1), channel_id=1, source_target_pairs={{0,4},{4,8},{8,12},{12,16},{16,20},{20,24},{24,28},{28,0},{1,5},{5... | collective-permute-start | bytes 786440 | tf_op jit(solution)/shard_map/ppermute | solution.py:27
  2.5 10.9 %collective-permute-start.5 = (bf16[16,64,128]{2,1,0:T(8,128)(2,1)}, bf16[16,64,128]{2,1,0:T(8,128)(2,1)S(1)}, u32[]{:S(2)}, u32[]{:S(2)}) collective-permute-start(bf16[16,64,128]{2,1,0:T(8,128)(2,1)} %refs_3_.1), channel_id=1, source_target_pairs={{4,0},{8,4},{12,8},{16,12},{20,16},{24,20},{28,24},{0,28},{5,1},{9... | collective-permute-start | bytes 786440 | tf_op jit(solution)/shard_map/ppermute | solution.py:30
  6.4 34.1 %collective-permute-start.9 = (bf16[16,64,384]{2,1,0:T(8,128)(2,1)}, bf16[16,64,384]{2,1,0:T(8,128)(2,1)S(1)}, u32[]{:S(2)}, u32[]{:S(2)}) collective-permute-start(bf16[16,64,384]{2,1,0:T(8,128)(2,1)} %refs_0_.1), channel_id=1, source_target_pairs={{0,4},{4,8},{8,12},{12,16},{16,20},{20,24},{24,28},{28,0},{1,5},{5... | collective-permute-start | bytes 2359304 | tf_op jit(solution)/shard_map/ppermute | solution.py:27
  6.4 34.1 %collective-permute-start.11 = (bf16[16,64,384]{2,1,0:T(8,128)(2,1)}, bf16[16,64,384]{2,1,0:T(8,128)(2,1)S(1)}, u32[]{:S(2)}, u32[]{:S(2)}) collective-permute-start(bf16[16,64,384]{2,1,0:T(8,128)(2,1)} %refs_0_.1), channel_id=1, source_target_pairs={{4,0},{8,4},{12,8},{16,12},{20,16},{24,20},{28,24},{0,28},{5,1},{9... | collective-permute-start | bytes 2359304 | tf_op jit(solution)/shard_map/ppermute | solution.py:30
  14.1 26.4 %collective-permute-start.16 = (bf16[48,64,128]{2,1,0:T(8,128)(2,1)}, bf16[48,64,128]{2,1,0:T(8,128)(2,1)S(1)}, u32[]{:S(2)}, u32[]{:S(2)}) collective-permute-start(bf16[48,64,128]{2,1,0:T(8,128)(2,1)} %constant_dynamic-update-slice_fusion.2), channel_id=1, source_target_pairs={{32,0},{64,32},{96,64},{128,96},{160,128},{192,160},{224,192},{33,... | collective-permute-start | bytes 2359304 | tf_op jit(solution)/shard_map/ppermute | solution.py:21
  18.1 22.4 %collective-permute-start.15 = (bf16[48,64,128]{2,1,0:T(8,128)(2,1)}, bf16[48,64,128]{2,1,0:T(8,128)(2,1)}, u32[]{:S(2)}, u32[]{:S(2)}) collective-permute-start(bf16[48,64,128]{2,1,0:T(8,128)(2,1)} %constant_dynamic-update-slice_fusion.2), channel_id=1, source_target_pairs={{0,32},{32,64},{64,96},{96,128},{128,160},{160,192},{192,224},{1,3... | collective-permute-start | bytes 2359304 | tf_op jit(solution)/shard_map/ppermute | solution.py:20
  23.3 17.2 %all-to-all-start = ((s32[32,1,128]{2,1,0:T(1,128)}), s32[32,1,128]{2,1,0:T(1,128)S(1)}, u32[]{:S(2)}, u32[]{:S(2)}) async-start(s32[32,1,128]{2,1,0:T(1,128)} %broadcast_in_dim.45), calls=%async_computation | async-start | bytes 32768 | tf_op jit(solution)/shard_map/all_to_all | solution.py:257
  48.6 42.6 %all-to-all-start.1 = ((bf16[4,6,64,768]{3,2,1,0:T(8,128)(2,1)}), bf16[4,6,64,768]{3,2,1,0:T(8,128)(2,1)}, u32[]{:S(2)}, u32[]{:S(2)}) async-start(bf16[4,6,64,768]{3,2,1,0:T(8,128)(2,1)} %bitcast.12), calls=%async_computation.1 | async-start | bytes 4718592 | tf_op jit(solution)/shard_map/all_to_all | solution.py:297
  53.2 7.6 %collective-permute-start.3 = (bf16[16,64,128]{2,1,0:T(8,128)(2,1)S(1)}, bf16[16,64,128]{2,1,0:T(8,128)(2,1)S(1)}, u32[]{:S(2)}, u32[]{:S(2)}) collective-permute-start(bf16[16,64,128]{2,1,0:T(8,128)(2,1)S(1)} %collective-permute-done.2.refs_4_), channel_id=1, source_target_pairs={{0,4},{4,8},{8,12},{12,16},{16,20},{20,24},{24,28},{28,0},{1,5},{5... | collective-permute-start | bytes 786440 | tf_op jit(solution)/shard_map/ppermute | solution.py:27
  53.6 9.9 %collective-permute-start.6 = (bf16[16,64,128]{2,1,0:T(8,128)(2,1)S(1)}, bf16[16,64,128]{2,1,0:T(8,128)(2,1)S(1)}, u32[]{:S(2)}, u32[]{:S(2)}) collective-permute-start(bf16[16,64,128]{2,1,0:T(8,128)(2,1)S(1)} %collective-permute-done.5.refs_5_), channel_id=1, source_target_pairs={{4,0},{8,4},{12,8},{16,12},{20,16},{24,20},{28,24},{0,28},{5,1},{9... | collective-permute-start | bytes 786440 | tf_op jit(solution)/shard_map/ppermute | solution.py:30
  60.8 25.2 %collective-permute-start.10 = (bf16[16,64,384]{2,1,0:T(8,128)(2,1)S(1)}, bf16[16,64,384]{2,1,0:T(8,128)(2,1)}, u32[]{:S(2)}, u32[]{:S(2)}) collective-permute-start(bf16[16,64,384]{2,1,0:T(8,128)(2,1)S(1)} %collective-permute-done.9.refs_1_), channel_id=1, source_target_pairs={{0,4},{4,8},{8,12},{12,16},{16,20},{20,24},{24,28},{28,0},{1,5},{5... | collective-permute-start | bytes 2359304 | tf_op jit(solution)/shard_map/ppermute | solution.py:27
  60.8 25.1 %collective-permute-start.12 = (bf16[16,64,384]{2,1,0:T(8,128)(2,1)S(1)}, bf16[16,64,384]{2,1,0:T(8,128)(2,1)S(1)}, u32[]{:S(2)}, u32[]{:S(2)}) collective-permute-start(bf16[16,64,384]{2,1,0:T(8,128)(2,1)S(1)} %collective-permute-done.11.refs_2_), channel_id=1, source_target_pairs={{4,0},{8,4},{12,8},{16,12},{20,16},{24,20},{28,24},{0,28},{5,1},{9... | collective-permute-start | bytes 2359304 | tf_op jit(solution)/shard_map/ppermute | solution.py:30
  63.6 20.9 %collective-permute-start.14 = (bf16[32,64,128]{2,1,0:T(8,128)(2,1)S(1)}, bf16[32,64,128]{2,1,0:T(8,128)(2,1)S(1)}, u32[]{:S(2)}, u32[]{:S(2)}) collective-permute-start(bf16[32,64,128]{2,1,0:T(8,128)(2,1)S(1)} %constant_dynamic-update-slice_fusion), channel_id=1, source_target_pairs={{32,0},{64,32},{96,64},{128,96},{160,128},{192,160},{224,192},{33,... | collective-permute-start | bytes 1572872 | tf_op jit(solution)/shard_map/ppermute | solution.py:21
  68.5 17.4 %collective-permute-start.13 = (bf16[32,64,128]{2,1,0:T(8,128)(2,1)S(1)}, bf16[32,64,128]{2,1,0:T(8,128)(2,1)S(1)}, u32[]{:S(2)}, u32[]{:S(2)}) collective-permute-start(bf16[32,64,128]{2,1,0:T(8,128)(2,1)S(1)} %constant_dynamic-update-slice_fusion), channel_id=1, source_target_pairs={{0,32},{32,64},{64,96},{96,128},{128,160},{160,192},{192,224},{1,3... | collective-permute-start | bytes 1572872 | tf_op jit(solution)/shard_map/ppermute | solution.py:20
  71.5 12.9 %collective-permute-start.4 = (bf16[16,64,128]{2,1,0:T(8,128)(2,1)S(1)}, bf16[16,64,128]{2,1,0:T(8,128)(2,1)S(1)}, u32[]{:S(2)}, u32[]{:S(2)}) collective-permute-start(bf16[16,64,128]{2,1,0:T(8,128)(2,1)S(1)} %collective-permute-done.3.refs_2_), channel_id=1, source_target_pairs={{0,4},{4,8},{8,12},{12,16},{16,20},{20,24},{24,28},{28,0},{1,5},{5... | collective-permute-start | bytes 786440 | tf_op jit(solution)/shard_map/ppermute | solution.py:27
  91.2 41.2 %all-to-all-start.2 = ((bf16[4,4,64,768]{3,2,1,0:T(8,128)(2,1)}), bf16[4,4,64,768]{3,2,1,0:T(8,128)(2,1)}, u32[]{:S(2)}, u32[]{:S(2)}) async-start(bf16[4,4,64,768]{3,2,1,0:T(8,128)(2,1)} %bitcast.11), calls=%async_computation.2 | async-start | bytes 3145728 | tf_op jit(solution)/shard_map/all_to_all | solution.py:297
  95.7 16.6 %collective-permute-start.17 = (bf16[16,64,384]{2,1,0:T(8,128)(2,1)}, bf16[16,64,384]{2,1,0:T(8,128)(2,1)S(1)}, u32[]{:S(2)}, u32[]{:S(2)}) collective-permute-start(bf16[16,64,384]{2,1,0:T(8,128)(2,1)} %collective-permute-done.10.refs_0_), channel_id=1, source_target_pairs={{0,4},{4,8},{8,12},{12,16},{16,20},{20,24},{24,28},{28,0},{1,5},{5... | collective-permute-start | bytes 2359304 | tf_op jit(solution)/shard_map/ppermute | solution.py:27
  96.0 18.5 %collective-permute-start.20 = (bf16[48,64,128]{2,1,0:T(8,128)(2,1)S(1)}, bf16[48,64,128]{2,1,0:T(8,128)(2,1)S(1)}, u32[]{:S(2)}, u32[]{:S(2)}) collective-permute-start(bf16[48,64,128]{2,1,0:T(8,128)(2,1)S(1)} %constant_dynamic-update-slice_fusion.5), channel_id=1, source_target_pairs={{32,0},{64,32},{96,64},{128,96},{160,128},{192,160},{224,192},{33,... | collective-permute-start | bytes 2359304 | tf_op jit(solution)/shard_map/ppermute | solution.py:21
  102.7 12.8 %collective-permute-start.19 = (bf16[48,64,128]{2,1,0:T(8,128)(2,1)S(1)}, bf16[48,64,128]{2,1,0:T(8,128)(2,1)S(1)}, u32[]{:S(2)}, u32[]{:S(2)}) collective-permute-start(bf16[48,64,128]{2,1,0:T(8,128)(2,1)S(1)} %constant_dynamic-update-slice_fusion.5), channel_id=1, source_target_pairs={{0,32},{32,64},{64,96},{96,128},{128,160},{160,192},{192,224},{1,3... | collective-permute-start | bytes 2359304 | tf_op jit(solution)/shard_map/ppermute | solution.py:20
  106.5 19.0 %collective-permute-start.18 = (bf16[16,64,384]{2,1,0:T(8,128)(2,1)}, bf16[16,64,384]{2,1,0:T(8,128)(2,1)S(1)}, u32[]{:S(2)}, u32[]{:S(2)}) collective-permute-start(bf16[16,64,384]{2,1,0:T(8,128)(2,1)} %copy-done.6), channel_id=1, source_target_pairs={{4,0},{8,4},{12,8},{16,12},{20,16},{24,20},{28,24},{0,28},{5,1},{9... | collective-permute-start | bytes 2359304 | tf_op jit(solution)/shard_map/ppermute | solution.py:30
  132.4 25.8 %all-to-all-start.3 = ((bf16[4,4,64,768]{3,2,1,0:T(8,128)(2,1)}), bf16[4,4,64,768]{3,2,1,0:T(8,128)(2,1)}, u32[]{:S(2)}, u32[]{:S(2)}) async-start(bf16[4,4,64,768]{3,2,1,0:T(8,128)(2,1)} %bitcast.13), calls=%async_computation.3 | async-start | bytes 3145728 | tf_op jit(solution)/shard_map/all_to_all | solution.py:297
  136.9 12.3 %collective-permute-start.21 = (bf16[8,64,384]{2,1,0:T(8,128)(2,1)S(1)}, bf16[8,64,384]{2,1,0:T(8,128)(2,1)S(1)}, u32[]{:S(2)}, u32[]{:S(2)}) collective-permute-start(bf16[8,64,384]{2,1,0:T(8,128)(2,1)S(1)} %slice.13), channel_id=1, source_target_pairs={{0,4},{4,8},{8,12},{12,16},{16,20},{20,24},{24,28},{28,0},{1,5},{5... | collective-permute-start | bytes 1179656 | tf_op jit(solution)/shard_map/ppermute | solution.py:27
  137.1 12.2 %collective-permute-start.22 = (bf16[8,64,384]{2,1,0:T(8,128)(2,1)S(1)}, bf16[8,64,384]{2,1,0:T(8,128)(2,1)S(1)}, u32[]{:S(2)}, u32[]{:S(2)}) collective-permute-start(bf16[8,64,384]{2,1,0:T(8,128)(2,1)S(1)} %slice.14), channel_id=1, source_target_pairs={{4,0},{8,4},{12,8},{16,12},{20,16},{24,20},{28,24},{0,28},{5,1},{9... | collective-permute-start | bytes 1179656 | tf_op jit(solution)/shard_map/ppermute | solution.py:30
  158.2 23.5 %all-to-all-start.4 = ((bf16[4,2,64,768]{3,2,1,0:T(8,128)(2,1)}), bf16[4,2,64,768]{3,2,1,0:T(8,128)(2,1)S(1)}, u32[]{:S(2)}, u32[]{:S(2)}) async-start(bf16[4,2,64,768]{3,2,1,0:T(8,128)(2,1)} %bitcast.14), calls=%async_computation.4 | async-start | bytes 1572864 | tf_op jit(solution)/shard_map/all_to_all | solution.py:319
  (13 other events, 179.0 us)

commit v3 on v2

--- a/solution.py
+++ b/solution.py
@@ -31,11 +31,13 @@
     return up, down
 
 
-def term_kernel(rows, nnz_a, nz, ny, offsets, pieces, first, meta, here, *refs):
+def term_kernel(rows, nnz_a, nz, ny, offsets, pieces, first, apart, meta, here, *refs):
     count = len(offsets)
     npieces = len(pieces)
     a_refs, p_refs = refs[:npieces], refs[npieces : npieces + count]
-    before, after, out, abuf, pall, apbuf, obuf, placed, listed, sems = refs[npieces + count :]
+    before, after = refs[npieces + count : npieces + count + 2]
+    outs = refs[npieces + count + 2 : -7]
+    abuf, pall, apbuf, obuf, placed, listed, sems = refs[-7:]
     copies = []
 
     def fetch(src, dst):
@@ -107,7 +109,8 @@
                 c = jnp.where(fits, c, 0)
                 place = placed[s * ny + c]
                 placed[s * ny + c] = place + jnp.where(fits, 1, 0)
-                slot = jnp.where(fits, c * (2 * count) + 2 * s + place, trash)
+                to = lax.rem(c - y + ny, ny) if apart else c
+                slot = jnp.where(fits, to * (2 * count) + 2 * s + place, trash)
                 obuf[slot] = t[p * BS : (p + 1) * BS]
         return 0
 
@@ -115,9 +118,15 @@
     for n in active[1:]:
         most = jnp.maximum(most, n)
     lax.fori_loop(0, most, row, 0)
-    copy = pltpu.make_async_copy(obuf.at[pl.ds(0, trash)], out, sems.at[0])
-    copy.start()
-    copy.wait()
+    size = trash // len(outs)
+    copies = [
+        pltpu.make_async_copy(obuf.at[pl.ds(i * size, size)], out, sems.at[i])
+        for i, out in enumerate(outs)
+    ]
+    for copy in copies:
+        copy.start()
+    for copy in copies:
+        copy.wait()
 
 
 def add_kernel(nseg, nz, ny, nnz_a, offsets, meta, slots, here, *refs):
@@ -171,7 +180,7 @@
             a = acc[seg * cells + 2 * h]
             b = acc[seg * cells + 2 * h + 1]
             v = jnp.where(low, a, b) + pltpu.roll(jnp.where(low, b, a), BS, 1)
-            stage[seg, :, 2 * BS * h : 2 * BS * (h + 1)] = v.astype(jnp.bfloat16)
+            stage[seg, :, 2 * BS * h : 2 * BS * (h + 1)] = v
         pltpu.make_async_copy(stage.at[seg], out.at[seg], sems.at[seg]).start()
         return 0
 
@@ -184,23 +193,22 @@
     lax.fori_loop(0, nseg, finish, 0)
 
 
-def last_kernel(nz, ny, nnz_a, offset, meta, slots, here, part, got, out, buf, stage, sems):
+def last_kernel(nseg, nz, ny, nnz_a, offsets, offset, meta, slots, here, part, got, *refs):
+    apart, out, acc, buf, late, stage, loadsems, sems = refs[:ny], *refs[ny:]
     cells = nz * ny
-    loads = [
-        pltpu.make_async_copy(part, stage, sems.at[0]),
-        pltpu.make_async_copy(got, buf, sems.at[1]),
-    ]
+    loads = [pltpu.make_async_copy(part, acc, loadsems.at[0])]
+    loads.append(pltpu.make_async_copy(got, buf, loadsems.at[1]))
+    for i in range(ny):
+        loads.append(pltpu.make_async_copy(apart[i], late.at[i], loadsems.at[2 + i]))
     for copy in loads:
         copy.start()
     for copy in loads:
         copy.wait()
     upper = lax.broadcasted_iota(jnp.int32, (BS, 2 * BS), 1) // BS
-    zs = lax.rem(here[0] + offset + nz, nz)
-
-    def slot(j, _):
-        y = j // 2
-        c = zs * ny + y
-        e = slots[2 * c + (j & 1)]
+    z, y = here[0], here[1]
+
+    def add(c, which, load):
+        e = slots[2 * c + which]
 
         @pl.when(e >= 0)
         def _():
@@ -210,22 +218,44 @@
                 far = w & 63
                 seg = w >> 6
                 src = (far >> 4) * (cells * 128) + c * 128 + (far & 15) * 8 + 6
-                x = buf[y, j & 1, :, 2 * BS * k : 2 * BS * (k + 1)].astype(jnp.float32)
+                x = load(slice(2 * BS * k, 2 * BS * (k + 1))).astype(jnp.float32)
                 turned_x = pltpu.roll(x, BS, 1)
                 for q in range(2):
                     cell = meta[src + q]
                     side = cell & 1
                     lanes = pl.ds(pl.multiple_of((cell >> 1) * (2 * BS), 2 * BS), 2 * BS)
                     v = jnp.where(upper == side, jnp.where(side == q, x, turned_x), 0.0)
-                    old = stage[seg, :, lanes].astype(jnp.float32)
-                    stage[seg, :, lanes] = (old + v).astype(jnp.bfloat16)
-
+                    acc[seg, :, lanes] = acc[seg, :, lanes] + v
+
+    for s, near in enumerate(offsets):
+        zs = lax.rem(z + near + nz, nz)
+
+        def slot(j, _, s=s, zs=zs):
+            add(zs * ny + j // 2, j & 1, lambda cols: buf[j // 2, 2 * s + (j & 1), :, cols])
+            return 0
+
+        lax.fori_loop(0, 2 * ny, slot, 0)
+    zs = lax.rem(z + offset + nz, nz)
+
+    def slot(j, _):
+        ys = lax.rem(y - j // 2 + ny, ny)
+        add(zs * ny + ys, j & 1, lambda cols: late[j // 2, j & 1, :, cols])
         return 0
 
     lax.fori_loop(0, 2 * ny, slot, 0)
-    copy = pltpu.make_async_copy(stage, out, sems.at[2])
-    copy.start()
-    copy.wait()
+
+    def put(seg, _):
+        stage[seg] = acc[seg].astype(jnp.bfloat16)
+        pltpu.make_async_copy(stage.at[seg], out.at[seg], sems.at[seg]).start()
+        return 0
+
+    lax.fori_loop(0, nseg, put, 0)
+
+    def finish(seg, _):
+        pltpu.make_async_copy(stage.at[seg], out.at[seg], sems.at[seg]).wait()
+        return 0
+
+    lax.fori_loop(0, nseg, finish, 0)
 
 
 def local(a_blocks, a_cols, p_blocks, p_cells):
@@ -297,11 +327,16 @@
             got.append(lax.all_to_all(sent, "y", 0, 0, tiled=True))
         pb, pa = near[batch]
         count = len(offsets)
+        apart = i == len(groups) - 1
+        parts_out = ny if apart else 1
+        shape = (ny * 2 * count // parts_out, BS, wide)
         sent = pl.pallas_call(
-            functools.partial(term_kernel, rows, nnz_a, nz, ny, offsets, pieces, start),
-            out_shape=jax.ShapeDtypeStruct((ny * 2 * count, BS, wide), jnp.bfloat16),
+            functools.partial(
+                term_kernel, rows, nnz_a, nz, ny, offsets, pieces, start, apart
+            ),
+            out_shape=[jax.ShapeDtypeStruct(shape, jnp.bfloat16)] * parts_out,
             in_specs=[SMEM, SMEM] + [ANY] * (len(a_list) + len(p_list) + 2),
-            out_specs=ANY,
+            out_specs=[ANY] * parts_out,
             scratch_shapes=[
                 pltpu.VMEM((count, rows, BS, nnz_a * BS), jnp.bfloat16),
                 pltpu.VMEM((count, 3 * rows, BS, 2 * BS), jnp.bfloat16),
@@ -309,26 +344,29 @@
                 pltpu.VMEM((ny * 2 * count + 1, BS, wide), jnp.bfloat16),
                 pltpu.SMEM((count * ny,), jnp.int32),
                 pltpu.SMEM((count * (rows + 1),), jnp.int32),
-                pltpu.SemaphoreType.DMA((len(pieces) + 3 * count,)),
+                pltpu.SemaphoreType.DMA((len(pieces) + 3 * count + ny,)),
             ],
             compiler_params=pltpu.CompilerParams(vmem_limit_bytes=24 << 20),
             name="terms",
         )(flat, here, *a_list, *p_list, pb, pa)
-        sent = sent.reshape(ny, 2 * count, BS, wide)
-    sent, got[-1] = lax.optimization_barrier((sent, got[-1]))
-    got.append(lax.all_to_all(sent, "y", 0, 0, tiled=True))
+        if apart:
+            break
+        sent = sent[0].reshape(ny, 2 * count, BS, wide)
+    late = [sent[0]]
+    for by in (1, 2, ny - 1):
+        late.append(lax.ppermute(sent[by], "y", [(i, (i + by) % ny) for i in range(ny)]))
     offsets = [g[0] for g in groups]
-    result = jax.ShapeDtypeStruct((nseg, BS, cells * BS), jnp.bfloat16)
+    shape = (nseg, BS, cells * BS)
     early = got[:-1]
     part = pl.pallas_call(
-        functools.partial(add_kernel, nseg, nz, ny, nnz_a, offsets[:-1]),
-        out_shape=result,
+        functools.partial(add_kernel, nseg, nz, ny, nnz_a, offsets[:-2]),
+        out_shape=jax.ShapeDtypeStruct(shape, jnp.float32),
         in_specs=[SMEM, SMEM, SMEM] + [ANY] * len(early),
         out_specs=ANY,
         scratch_shapes=[pltpu.VMEM(g.shape, g.dtype) for g in early]
         + [
             pltpu.VMEM((nseg * cells, BS, 2 * BS), jnp.float32),
-            pltpu.VMEM(result.shape, result.dtype),
+            pltpu.VMEM(shape, jnp.float32),
             pltpu.SemaphoreType.DMA((len(early),)),
             pltpu.SemaphoreType.DMA((nseg,)),
         ],
@@ -336,18 +374,21 @@
         name="add",
     )(three, slots, here, *early)
     out = pl.pallas_call(
-        functools.partial(last_kernel, nz, ny, nnz_a, half),
-        out_shape=result,
-        in_specs=[SMEM, SMEM, SMEM, ANY, ANY],
+        functools.partial(last_kernel, nseg, nz, ny, nnz_a, offsets[-2], half),
+        out_shape=jax.ShapeDtypeStruct(shape, jnp.bfloat16),
+        in_specs=[SMEM, SMEM, SMEM] + [ANY] * (2 + ny),
         out_specs=ANY,
         scratch_shapes=[
+            pltpu.VMEM(shape, jnp.float32),
             pltpu.VMEM(got[-1].shape, jnp.bfloat16),
-            pltpu.VMEM(result.shape, result.dtype),
-            pltpu.SemaphoreType.DMA((3,)),
+            pltpu.VMEM((ny, 2, BS, wide), jnp.bfloat16),
+            pltpu.VMEM(shape, jnp.bfloat16),
+            pltpu.SemaphoreType.DMA((2 + ny,)),
+            pltpu.SemaphoreType.DMA((nseg,)),
         ],
         compiler_params=pltpu.CompilerParams(vmem_limit_bytes=60 << 20),
         name="finish",
-    )(three, slots, here, part, got[-1])
+    )(three, slots, here, part, got[-1], *late)
     return out.reshape(coarse_here, 3, 3, BS, cells * BS)
 
 

time: 192 us -> 187 us (0.974)
  the two profiles are of different devices: /device:TPU:1 before, /device:TPU:2 now
where the time goes in v3:
time: 187 us; the launch traced here: 186 us
  starting transfers between devices  70.5 us (38%)
  waiting for transfers between devices  57 us (30%)
  Pallas kernels  44.5 us (24%)
  local copies, waits for them, and re-layouts  11.2 us (6%)
  other arithmetic  2.23 us (1%)
    ppermute x8, waiting for transfers between devices, turned(): up = lax.ppermute(up, 'z', [(i, (i + 1) % n) for i in range(n)])  39.3 us
    pallas_call x4, Pallas kernels, local(): pl.pallas_call(functools.partial(term_kernel, rows, nnz_a, nz, ny, offset...  20.6 us
    ppermute x7, starting transfers between devices, turned(): down = lax.ppermute(down, 'z', [((i + 1) % n, i) for i in range(n)])  18.8 us
    all_to_all x3, starting transfers between devices, local(): got.append(lax.all_to_all(sent, 'y', 0, 0, tiled=True))  13.7 us
    pallas_call x1, Pallas kernels, local(): pl.pallas_call(functools.partial(last_kernel, nseg, nz, ny, nnz_a, offset...  12.5 us
    pallas_call x1, Pallas kernels, local(): pl.pallas_call(functools.partial(add_kernel, nseg, nz, ny, nnz_a, offsets...  11.4 us
    all_to_all x1, waiting for transfers between devices, local(): lax.all_to_all(jnp.broadcast_to(meta[None], (cells, rows * 8)), ('z', 'y'...  9.69 us
    ppermute x4, starting transfers between devices, shifted(): before = lax.ppermute(value, 'frame', [(i, i + 1) for i in range(n - 1)])  9.63 us
  transfers between devices with their start and end apart: 30, of which 9 were waited for; matrix products, arithmetic and copies ran while one was open for 5% of the time, Pallas kernels for 14%

profile of v3, /device:TPU:2, one launch (start us, length us, event | category | flops | bytes accessed | tf_op | source)
XLA Modules:
  0.0 186.0 jit_solution(10766309029061500855)
XLA Ops:
  1.9 3.9 %collective-permute-start.5 = (bf16[16,64,128]{2,1,0:T(8,128)(2,1)}, bf16[16,64,128]{2,1,0:T(8,128)(2,1)S(1)}, u32[]{:S(2)}, u32[]{:S(2)}) collective-permute-start(bf16[16,64,128]{2,1,0:T(8,128)(2,1)} %refs_3_.1), channel_id=1, source_target_pairs={{4,0},{8,4},{12,8},{16,12},{20,16},{24,20},{28,24},{0,28},{5,1},{9... | collective-permute-start | bytes 786440 | tf_op jit(solution)/shard_map/ppermute | solution.py:30
  5.9 3.2 %collective-permute-start.11 = (bf16[16,64,384]{2,1,0:T(8,128)(2,1)}, bf16[16,64,384]{2,1,0:T(8,128)(2,1)S(1)}, u32[]{:S(2)}, u32[]{:S(2)}) collective-permute-start(bf16[16,64,384]{2,1,0:T(8,128)(2,1)} %refs_0_.1), channel_id=1, source_target_pairs={{4,0},{8,4},{12,8},{16,12},{20,16},{24,20},{28,24},{0,28},{5,1},{9... | collective-permute-start | bytes 2359304 | tf_op jit(solution)/shard_map/ppermute | solution.py:30
  10.8 2.5 %collective-permute-done.2.refs_4_ = bf16[16,64,128]{2,1,0:T(8,128)(2,1)S(1)} collective-permute-done((bf16[16,64,128]{2,1,0:T(8,128)(2,1)}, bf16[16,64,128]{2,1,0:T(8,128)(2,1)S(1)}, u32[]{:S(2)}, u32[]{:S(2)}) %collective-permute-start.2) | collective-permute-done | bytes 262176 | tf_op jit(solution)/shard_map/ppermute | solution.py:27
  21.2 8.9 %all-to-all-start = ((s32[32,1,128]{2,1,0:T(1,128)}), s32[32,1,128]{2,1,0:T(1,128)S(1)}, u32[]{:S(2)}, u32[]{:S(2)}) async-start(s32[32,1,128]{2,1,0:T(1,128)} %broadcast_in_dim.45), calls=%async_computation | async-start | bytes 32768 | tf_op jit(solution)/shard_map/all_to_all | solution.py:287
  30.1 9.7 %all-to-all-done = s32[32,1,128]{2,1,0:T(1,128)S(1)} async-done(((s32[32,1,128]{2,1,0:T(1,128)}), s32[32,1,128]{2,1,0:T(1,128)S(1)}, u32[]{:S(2)}, u32[]{:S(2)}) %all-to-all-start) | async-done | bytes 16416 | tf_op jit(solution)/shard_map/all_to_all | solution.py:287
  41.9 6.0 %terms.5 = bf16[24,64,768]{2,1,0:T(8,128)(2,1)} custom-call(s32[4096]{0:T(1024)S(1)} %bitcast.18, s32[2]{0:T(128)S(1)} %pad_add_fusion.3.here, bf16[16,64,384]{2,1,0:T(8,128)(2,1)S(1)} %copy-done.5, bf16[16,64,384]{2,1,0:T(8,128)(2,1)S(1)} %collective-permute-done.9.refs_1_, bf16[16,64,384]{2,1,0:T(8,128)(2,1)S(1)} %collective-permute-done.11.refs_2_, ...), custom_call_target="tpu_custom_call" | custom-call | tf_op jit(solution)/shard_map/terms/pallas_call | solution.py:333
  48.0 4.5 %all-to-all-start.1 = ((bf16[4,6,64,768]{3,2,1,0:T(8,128)(2,1)}), bf16[4,6,64,768]{3,2,1,0:T(8,128)(2,1)}, u32[]{:S(2)}, u32[]{:S(2)}) async-start(bf16[4,6,64,768]{3,2,1,0:T(8,128)(2,1)} %bitcast.12), calls=%async_computation.1 | async-start | bytes 4718592 | tf_op jit(solution)/shard_map/all_to_all | solution.py:327
  53.3 2.6 %collective-permute-start.6 = (bf16[16,64,128]{2,1,0:T(8,128)(2,1)S(1)}, bf16[16,64,128]{2,1,0:T(8,128)(2,1)S(1)}, u32[]{:S(2)}, u32[]{:S(2)}) collective-permute-start(bf16[16,64,128]{2,1,0:T(8,128)(2,1)S(1)} %collective-permute-done.5.refs_5_), channel_id=1, source_target_pairs={{4,0},{8,4},{12,8},{16,12},{20,16},{24,20},{28,24},{0,28},{5,1},{9... | collective-permute-start | bytes 786440 | tf_op jit(solution)/shard_map/ppermute | solution.py:30
  55.8 5.7 %collective-permute-done.3.refs_2_ = bf16[16,64,128]{2,1,0:T(8,128)(2,1)S(1)} collective-permute-done((bf16[16,64,128]{2,1,0:T(8,128)(2,1)S(1)}, bf16[16,64,128]{2,1,0:T(8,128)(2,1)S(1)}, u32[]{:S(2)}, u32[]{:S(2)}) %collective-permute-start.3) | collective-permute-done | bytes 262176 | tf_op jit(solution)/shard_map/ppermute | solution.py:27
  61.6 3.2 %collective-permute-start.12 = (bf16[16,64,384]{2,1,0:T(8,128)(2,1)S(1)}, bf16[16,64,384]{2,1,0:T(8,128)(2,1)S(1)}, u32[]{:S(2)}, u32[]{:S(2)}) collective-permute-start(bf16[16,64,384]{2,1,0:T(8,128)(2,1)S(1)} %collective-permute-done.11.refs_2_), channel_id=1, source_target_pairs={{4,0},{8,4},{12,8},{16,12},{20,16},{24,20},{28,24},{0,28},{5,1},{9... | collective-permute-start | bytes 2359304 | tf_op jit(solution)/shard_map/ppermute | solution.py:30
  69.3 17.3 %collective-permute-done.4.refs_2_ = bf16[16,64,128]{2,1,0:T(8,128)(2,1)S(1)} collective-permute-done((bf16[16,64,128]{2,1,0:T(8,128)(2,1)S(1)}, bf16[16,64,128]{2,1,0:T(8,128)(2,1)S(1)}, u32[]{:S(2)}, u32[]{:S(2)}) %collective-permute-start.4) | collective-permute-done | bytes 262176 | tf_op jit(solution)/shard_map/ppermute | solution.py:27
  88.7 5.3 %terms.4 = bf16[16,64,768]{2,1,0:T(8,128)(2,1)} custom-call(s32[4096]{0:T(1024)S(1)} %bitcast.19, s32[2]{0:T(128)S(1)} %pad_add_fusion.3.here, bf16[16,64,384]{2,1,0:T(8,128)(2,1)} %collective-permute-done.10.refs_0_, bf16[16,64,384]{2,1,0:T(8,128)(2,1)S(1)} %collective-permute-done.12.refs_1_, bf16[16,64,128]{2,1,0:T(8,128)(2,1)S(1)} %collective-permute-done.3.refs_2_, ...), custom_call_target="tpu_custom_call" | custom-call | tf_op jit(solution)/shard_map/terms/pallas_call | solution.py:333
  94.3 4.4 %all-to-all-start.2 = ((bf16[4,4,64,768]{3,2,1,0:T(8,128)(2,1)}), bf16[4,4,64,768]{3,2,1,0:T(8,128)(2,1)}, u32[]{:S(2)}, u32[]{:S(2)}) async-start(bf16[4,4,64,768]{3,2,1,0:T(8,128)(2,1)} %bitcast.11), calls=%async_computation.2 | async-start | bytes 3145728 | tf_op jit(solution)/shard_map/all_to_all | solution.py:327
  104.2 2.6 %collective-permute-start.18 = (bf16[16,64,384]{2,1,0:T(8,128)(2,1)}, bf16[16,64,384]{2,1,0:T(8,128)(2,1)S(1)}, u32[]{:S(2)}, u32[]{:S(2)}) collective-permute-start(bf16[16,64,384]{2,1,0:T(8,128)(2,1)} %copy-done.6), channel_id=1, source_target_pairs={{4,0},{8,4},{12,8},{16,12},{20,16},{24,20},{28,24},{0,28},{5,1},{9... | collective-permute-start | bytes 2359304 | tf_op jit(solution)/shard_map/ppermute | solution.py:30
  106.8 10.1 %collective-permute-done.17.refs_0_ = bf16[16,64,384]{2,1,0:T(8,128)(2,1)S(1)} collective-permute-done((bf16[16,64,384]{2,1,0:T(8,128)(2,1)}, bf16[16,64,384]{2,1,0:T(8,128)(2,1)S(1)}, u32[]{:S(2)}, u32[]{:S(2)}) %collective-permute-start.17) | collective-permute-done | bytes 786464 | tf_op jit(solution)/shard_map/ppermute | solution.py:27
  116.9 7.7 %collective-permute-done.18.refs_1_ = bf16[16,64,384]{2,1,0:T(8,128)(2,1)S(1)} collective-permute-done((bf16[16,64,384]{2,1,0:T(8,128)(2,1)}, bf16[16,64,384]{2,1,0:T(8,128)(2,1)S(1)}, u32[]{:S(2)}, u32[]{:S(2)}) %collective-permute-start.18) | collective-permute-done | bytes 786464 | tf_op jit(solution)/shard_map/ppermute | solution.py:30
  126.5 5.0 %terms.6 = bf16[16,64,768]{2,1,0:T(8,128)(2,1)} custom-call(s32[4096]{0:T(1024)S(1)} %bitcast.20, s32[2]{0:T(128)S(1)} %pad_add_fusion.3.here, bf16[16,64,384]{2,1,0:T(8,128)(2,1)S(1)} %collective-permute-done.17.refs_0_, bf16[16,64,384]{2,1,0:T(8,128)(2,1)S(1)} %collective-permute-done.18.refs_1_, bf16[16,64,128]{2,1,0:T(8,128)(2,1)S(1)} %copy-done.2, ...), custom_call_target="tpu_custom_call" | custom-call | tf_op jit(solution)/shard_map/terms/pallas_call | solution.py:333
  131.5 4.8 %all-to-all-start.3 = ((bf16[4,4,64,768]{3,2,1,0:T(8,128)(2,1)}), bf16[4,4,64,768]{3,2,1,0:T(8,128)(2,1)}, u32[]{:S(2)}, u32[]{:S(2)}) async-start(bf16[4,4,64,768]{3,2,1,0:T(8,128)(2,1)} %bitcast.13), calls=%async_computation.3 | async-start | bytes 3145728 | tf_op jit(solution)/shard_map/all_to_all | solution.py:327
  137.8 3.2 %collective-permute-start.22 = (bf16[8,64,384]{2,1,0:T(8,128)(2,1)}, bf16[8,64,384]{2,1,0:T(8,128)(2,1)S(1)}, u32[]{:S(2)}, u32[]{:S(2)}) collective-permute-start(bf16[8,64,384]{2,1,0:T(8,128)(2,1)} %slice.14), channel_id=1, source_target_pairs={{4,0},{8,4},{12,8},{16,12},{20,16},{24,20},{28,24},{0,28},{5,1},{9... | collective-permute-start | bytes 1179656 | tf_op jit(solution)/shard_map/ppermute | solution.py:30
  145.6 3.5 %collective-permute-done.21.refs_0_ = bf16[8,64,384]{2,1,0:T(8,128)(2,1)S(1)} collective-permute-done((bf16[8,64,384]{2,1,0:T(8,128)(2,1)}, bf16[8,64,384]{2,1,0:T(8,128)(2,1)S(1)}, u32[]{:S(2)}, u32[]{:S(2)}) %collective-permute-start.21) | collective-permute-done | bytes 393248 | tf_op jit(solution)/shard_map/ppermute | solution.py:27
  149.3 4.4 %terms.7 = (bf16[2,64,768]{2,1,0:T(8,128)(2,1)S(1)}, bf16[2,64,768]{2,1,0:T(8,128)(2,1)S(1)}, bf16[2,64,768]{2,1,0:T(8,128)(2,1)S(1)}, bf16[2,64,768]{2,1,0:T(8,128)(2,1)S(1)}) custom-call(s32[4096]{0:T(1024)S(1)} %bitcast.23, s32[2]{0:T(128)S(1)} %pad_add_fusion.3.here, bf16[8,64,384]{2,1,0:T(8,128)(2,1)S(1)} %collective-permute-done.21.refs_0_, ...), custom_call_target="tpu_custom_call" | custom-call | tf_op jit(solution)/shard_map/terms/pallas_call | solution.py:333
  155.5 2.8 %collective-permute-start.24 = (bf16[2,64,768]{2,1,0:T(8,128)(2,1)S(1)}, bf16[2,64,768]{2,1,0:T(8,128)(2,1)S(1)}, u32[]{:S(2)}, u32[]{:S(2)}) collective-permute-start(bf16[2,64,768]{2,1,0:T(8,128)(2,1)S(1)} %get-tuple-element.27), channel_id=1, source_target_pairs={{0,2},{1,3},{2,0},{3,1},{4,6},{5,7},{6,4},{7,5},{8,10},{9,11},{10,... | collective-permute-start | bytes 589832 | tf_op jit(solution)/shard_map/ppermute | solution.py:357
  161.1 11.4 %add.81.part = f32[18,64,2048]{2,1,0:T(8,128)} custom-call(s32[12288]{0:T(1024)} %bitcast.25, s32[64]{0:T(128)} %reshape.114.slots, s32[2]{0:T(128)} %copy-done.8, bf16[4,6,64,768]{3,2,1,0:T(8,128)(2,1)} %all-to-all-done.1.refs_0_, bf16[4,4,64,768]{3,2,1,0:T(8,128)(2,1)} %all-to-all-done.2.refs_1_), custom_call_target="tpu_custom_call" | custom-call | tf_op jit(solution)/shard_map/add/pallas_call | solution.py:361
  173.3 12.5 %finish.1 = bf16[18,64,2048]{2,1,0:T(8,128)(2,1)} custom-call(s32[12288]{0:T(1024)} %bitcast.26, s32[64]{0:T(128)} %reshape.114.slots, s32[2]{0:T(128)} %copy-done.8, f32[18,64,2048]{2,1,0:T(8,128)} %add.81.part, bf16[4,4,64,768]{3,2,1,0:T(8,128)(2,1)} %all-to-all-done.3.got, bf16[2,64,768]{2,1,0:T(8,128)(2,1)} %copy-done.7, bf16[2,64,768]{2,1,0:T(8,128)(2,1)} %copy-done.9, ...), custom_call_target="tpu_custom_call" | custom-call | tf_op jit(solution)/shard_map/finish/pallas_call | solution.py:376
  (91 shorter events, 40.4 us)
Async XLA Ops:
  0.0 13.2 %collective-permute-start.2 = (bf16[16,64,128]{2,1,0:T(8,128)(2,1)}, bf16[16,64,128]{2,1,0:T(8,128)(2,1)S(1)}, u32[]{:S(2)}, u32[]{:S(2)}) collective-permute-start(bf16[16,64,128]{2,1,0:T(8,128)(2,1)} %refs_3_.1), channel_id=1, source_target_pairs={{0,4},{4,8},{8,12},{12,16},{16,20},{20,24},{24,28},{28,0},{1,5},{5... | collective-permute-start | bytes 786440 | tf_op jit(solution)/shard_map/ppermute | solution.py:27
  5.9 34.0 %collective-permute-start.9 = (bf16[16,64,384]{2,1,0:T(8,128)(2,1)}, bf16[16,64,384]{2,1,0:T(8,128)(2,1)S(1)}, u32[]{:S(2)}, u32[]{:S(2)}) collective-permute-start(bf16[16,64,384]{2,1,0:T(8,128)(2,1)} %refs_0_.1), channel_id=1, source_target_pairs={{0,4},{4,8},{8,12},{12,16},{16,20},{20,24},{24,28},{28,0},{1,5},{5... | collective-permute-start | bytes 2359304 | tf_op jit(solution)/shard_map/ppermute | solution.py:27
  5.9 34.0 %collective-permute-start.11 = (bf16[16,64,384]{2,1,0:T(8,128)(2,1)}, bf16[16,64,384]{2,1,0:T(8,128)(2,1)S(1)}, u32[]{:S(2)}, u32[]{:S(2)}) collective-permute-start(bf16[16,64,384]{2,1,0:T(8,128)(2,1)} %refs_0_.1), channel_id=1, source_target_pairs={{4,0},{8,4},{12,8},{16,12},{20,16},{24,20},{28,24},{0,28},{5,1},{9... | collective-permute-start | bytes 2359304 | tf_op jit(solution)/shard_map/ppermute | solution.py:30
  14.7 25.2 %collective-permute-start.16 = (bf16[48,64,128]{2,1,0:T(8,128)(2,1)}, bf16[48,64,128]{2,1,0:T(8,128)(2,1)S(1)}, u32[]{:S(2)}, u32[]{:S(2)}) collective-permute-start(bf16[48,64,128]{2,1,0:T(8,128)(2,1)} %constant_dynamic-update-slice_fusion.2), channel_id=1, source_target_pairs={{32,0},{64,32},{96,64},{128,96},{160,128},{192,160},{224,192},{33,... | collective-permute-start | bytes 2359304 | tf_op jit(solution)/shard_map/ppermute | solution.py:21
  16.6 23.3 %collective-permute-start.15 = (bf16[48,64,128]{2,1,0:T(8,128)(2,1)}, bf16[48,64,128]{2,1,0:T(8,128)(2,1)}, u32[]{:S(2)}, u32[]{:S(2)}) collective-permute-start(bf16[48,64,128]{2,1,0:T(8,128)(2,1)} %constant_dynamic-update-slice_fusion.2), channel_id=1, source_target_pairs={{0,32},{32,64},{64,96},{96,128},{128,160},{160,192},{192,224},{1,3... | collective-permute-start | bytes 2359304 | tf_op jit(solution)/shard_map/ppermute | solution.py:20
  21.2 18.6 %all-to-all-start = ((s32[32,1,128]{2,1,0:T(1,128)}), s32[32,1,128]{2,1,0:T(1,128)S(1)}, u32[]{:S(2)}, u32[]{:S(2)}) async-start(s32[32,1,128]{2,1,0:T(1,128)} %broadcast_in_dim.45), calls=%async_computation | async-start | bytes 32768 | tf_op jit(solution)/shard_map/all_to_all | solution.py:287
  48.0 46.4 %all-to-all-start.1 = ((bf16[4,6,64,768]{3,2,1,0:T(8,128)(2,1)}), bf16[4,6,64,768]{3,2,1,0:T(8,128)(2,1)}, u32[]{:S(2)}, u32[]{:S(2)}) async-start(bf16[4,6,64,768]{3,2,1,0:T(8,128)(2,1)} %bitcast.12), calls=%async_computation.1 | async-start | bytes 4718592 | tf_op jit(solution)/shard_map/all_to_all | solution.py:327
  61.6 27.2 %collective-permute-start.10 = (bf16[16,64,384]{2,1,0:T(8,128)(2,1)S(1)}, bf16[16,64,384]{2,1,0:T(8,128)(2,1)}, u32[]{:S(2)}, u32[]{:S(2)}) collective-permute-start(bf16[16,64,384]{2,1,0:T(8,128)(2,1)S(1)} %collective-permute-done.9.refs_1_), channel_id=1, source_target_pairs={{0,4},{4,8},{8,12},{12,16},{16,20},{20,24},{24,28},{28,0},{1,5},{5... | collective-permute-start | bytes 2359304 | tf_op jit(solution)/shard_map/ppermute | solution.py:27
  61.6 27.1 %collective-permute-start.12 = (bf16[16,64,384]{2,1,0:T(8,128)(2,1)S(1)}, bf16[16,64,384]{2,1,0:T(8,128)(2,1)S(1)}, u32[]{:S(2)}, u32[]{:S(2)}) collective-permute-start(bf16[16,64,384]{2,1,0:T(8,128)(2,1)S(1)} %collective-permute-done.11.refs_2_), channel_id=1, source_target_pairs={{4,0},{8,4},{12,8},{16,12},{20,16},{24,20},{28,24},{0,28},{5,1},{9... | collective-permute-start | bytes 2359304 | tf_op jit(solution)/shard_map/ppermute | solution.py:30
  64.9 21.8 %collective-permute-start.14 = (bf16[32,64,128]{2,1,0:T(8,128)(2,1)S(1)}, bf16[32,64,128]{2,1,0:T(8,128)(2,1)S(1)}, u32[]{:S(2)}, u32[]{:S(2)}) collective-permute-start(bf16[32,64,128]{2,1,0:T(8,128)(2,1)S(1)} %constant_dynamic-update-slice_fusion), channel_id=1, source_target_pairs={{32,0},{64,32},{96,64},{128,96},{160,128},{192,160},{224,192},{33,... | collective-permute-start | bytes 1572872 | tf_op jit(solution)/shard_map/ppermute | solution.py:21
  66.8 21.9 %collective-permute-start.13 = (bf16[32,64,128]{2,1,0:T(8,128)(2,1)S(1)}, bf16[32,64,128]{2,1,0:T(8,128)(2,1)S(1)}, u32[]{:S(2)}, u32[]{:S(2)}) collective-permute-start(bf16[32,64,128]{2,1,0:T(8,128)(2,1)S(1)} %constant_dynamic-update-slice_fusion), channel_id=1, source_target_pairs={{0,32},{32,64},{64,96},{96,128},{128,160},{160,192},{192,224},{1,3... | collective-permute-start | bytes 1572872 | tf_op jit(solution)/shard_map/ppermute | solution.py:20
  69.3 17.4 %collective-permute-start.4 = (bf16[16,64,128]{2,1,0:T(8,128)(2,1)S(1)}, bf16[16,64,128]{2,1,0:T(8,128)(2,1)S(1)}, u32[]{:S(2)}, u32[]{:S(2)}) collective-permute-start(bf16[16,64,128]{2,1,0:T(8,128)(2,1)S(1)} %collective-permute-done.3.refs_2_), channel_id=1, source_target_pairs={{0,4},{4,8},{8,12},{12,16},{16,20},{20,24},{24,28},{28,0},{1,5},{5... | collective-permute-start | bytes 786440 | tf_op jit(solution)/shard_map/ppermute | solution.py:27
  94.3 37.1 %all-to-all-start.2 = ((bf16[4,4,64,768]{3,2,1,0:T(8,128)(2,1)}), bf16[4,4,64,768]{3,2,1,0:T(8,128)(2,1)}, u32[]{:S(2)}, u32[]{:S(2)}) async-start(bf16[4,4,64,768]{3,2,1,0:T(8,128)(2,1)} %bitcast.11), calls=%async_computation.2 | async-start | bytes 3145728 | tf_op jit(solution)/shard_map/all_to_all | solution.py:327
  98.9 18.0 %collective-permute-start.17 = (bf16[16,64,384]{2,1,0:T(8,128)(2,1)}, bf16[16,64,384]{2,1,0:T(8,128)(2,1)S(1)}, u32[]{:S(2)}, u32[]{:S(2)}) collective-permute-start(bf16[16,64,384]{2,1,0:T(8,128)(2,1)} %collective-permute-done.10.refs_0_), channel_id=1, source_target_pairs={{0,4},{4,8},{8,12},{12,16},{16,20},{20,24},{24,28},{28,0},{1,5},{5... | collective-permute-start | bytes 2359304 | tf_op jit(solution)/shard_map/ppermute | solution.py:27
  99.7 17.2 %collective-permute-start.20 = (bf16[48,64,128]{2,1,0:T(8,128)(2,1)S(1)}, bf16[48,64,128]{2,1,0:T(8,128)(2,1)S(1)}, u32[]{:S(2)}, u32[]{:S(2)}) collective-permute-start(bf16[48,64,128]{2,1,0:T(8,128)(2,1)S(1)} %constant_dynamic-update-slice_fusion.5), channel_id=1, source_target_pairs={{32,0},{64,32},{96,64},{128,96},{160,128},{192,160},{224,192},{33,... | collective-permute-start | bytes 2359304 | tf_op jit(solution)/shard_map/ppermute | solution.py:21
  101.8 15.1 %collective-permute-start.19 = (bf16[48,64,128]{2,1,0:T(8,128)(2,1)S(1)}, bf16[48,64,128]{2,1,0:T(8,128)(2,1)S(1)}, u32[]{:S(2)}, u32[]{:S(2)}) collective-permute-start(bf16[48,64,128]{2,1,0:T(8,128)(2,1)S(1)} %constant_dynamic-update-slice_fusion.5), channel_id=1, source_target_pairs={{0,32},{32,64},{64,96},{96,128},{128,160},{160,192},{192,224},{1,3... | collective-permute-start | bytes 2359304 | tf_op jit(solution)/shard_map/ppermute | solution.py:20
  104.2 20.4 %collective-permute-start.18 = (bf16[16,64,384]{2,1,0:T(8,128)(2,1)}, bf16[16,64,384]{2,1,0:T(8,128)(2,1)S(1)}, u32[]{:S(2)}, u32[]{:S(2)}) collective-permute-start(bf16[16,64,384]{2,1,0:T(8,128)(2,1)} %copy-done.6), channel_id=1, source_target_pairs={{4,0},{8,4},{12,8},{16,12},{20,16},{24,20},{28,24},{0,28},{5,1},{9... | collective-permute-start | bytes 2359304 | tf_op jit(solution)/shard_map/ppermute | solution.py:30
  131.5 41.1 %all-to-all-start.3 = ((bf16[4,4,64,768]{3,2,1,0:T(8,128)(2,1)}), bf16[4,4,64,768]{3,2,1,0:T(8,128)(2,1)}, u32[]{:S(2)}, u32[]{:S(2)}) async-start(bf16[4,4,64,768]{3,2,1,0:T(8,128)(2,1)} %bitcast.13), calls=%async_computation.3 | async-start | bytes 3145728 | tf_op jit(solution)/shard_map/all_to_all | solution.py:327
  137.0 12.1 %collective-permute-start.21 = (bf16[8,64,384]{2,1,0:T(8,128)(2,1)}, bf16[8,64,384]{2,1,0:T(8,128)(2,1)S(1)}, u32[]{:S(2)}, u32[]{:S(2)}) collective-permute-start(bf16[8,64,384]{2,1,0:T(8,128)(2,1)} %slice.13), channel_id=1, source_target_pairs={{0,4},{4,8},{8,12},{12,16},{16,20},{20,24},{24,28},{28,0},{1,5},{5... | collective-permute-start | bytes 1179656 | tf_op jit(solution)/shard_map/ppermute | solution.py:27
  141.1 19.4 %collective-permute-start.1 = (s32[32,128]{1,0:T(8,128)S(1)}, s32[32,128]{1,0:T(8,128)S(1)}, u32[]{:S(2)}, u32[]{:S(2)}) collective-permute-start(s32[32,128]{1,0:T(8,128)S(1)} %bitcast.21), channel_id=1, source_target_pairs={{32,0},{64,32},{96,64},{128,96},{160,128},{192,160},{224,192},{33,... | collective-permute-start | bytes 49160 | tf_op jit(solution)/shard_map/ppermute | solution.py:21
  143.0 17.5 %collective-permute-start = (s32[32,128]{1,0:T(8,128)S(1)}, s32[32,128]{1,0:T(8,128)S(1)}, u32[]{:S(2)}, u32[]{:S(2)}) collective-permute-start(s32[32,128]{1,0:T(8,128)S(1)} %bitcast.22), channel_id=1, source_target_pairs={{0,32},{32,64},{64,96},{96,128},{128,160},{160,192},{192,224},{1,3... | collective-permute-start | bytes 49160 | tf_op jit(solution)/shard_map/ppermute | solution.py:20
  153.7 18.8 %collective-permute-start.23 = (bf16[2,64,768]{2,1,0:T(8,128)(2,1)S(1)}, bf16[2,64,768]{2,1,0:T(8,128)(2,1)S(1)}, u32[]{:S(2)}, u32[]{:S(2)}) collective-permute-start(bf16[2,64,768]{2,1,0:T(8,128)(2,1)S(1)} %get-tuple-element.26), channel_id=1, source_target_pairs={{0,1},{1,2},{2,3},{3,0},{4,5},{5,6},{6,7},{7,4},{8,9},{9,10},{10,1... | collective-permute-start | bytes 589832 | tf_op jit(solution)/shard_map/ppermute | solution.py:357
  155.5 17.0 %collective-permute-start.24 = (bf16[2,64,768]{2,1,0:T(8,128)(2,1)S(1)}, bf16[2,64,768]{2,1,0:T(8,128)(2,1)S(1)}, u32[]{:S(2)}, u32[]{:S(2)}) collective-permute-start(bf16[2,64,768]{2,1,0:T(8,128)(2,1)S(1)} %get-tuple-element.27), channel_id=1, source_target_pairs={{0,2},{1,3},{2,0},{3,1},{4,6},{5,7},{6,4},{7,5},{8,10},{9,11},{10,... | collective-permute-start | bytes 589832 | tf_op jit(solution)/shard_map/ppermute | solution.py:357
  158.3 14.2 %collective-permute-start.25 = (bf16[2,64,768]{2,1,0:T(8,128)(2,1)S(1)}, bf16[2,64,768]{2,1,0:T(8,128)(2,1)S(1)}, u32[]{:S(2)}, u32[]{:S(2)}) collective-permute-start(bf16[2,64,768]{2,1,0:T(8,128)(2,1)S(1)} %get-tuple-element.28), channel_id=1, source_target_pairs={{0,3},{1,0},{2,1},{3,2},{4,7},{5,4},{6,5},{7,6},{8,11},{9,8},{10,9... | collective-permute-start | bytes 589832 | tf_op jit(solution)/shard_map/ppermute | solution.py:357
  (18 other events, 233.2 us)

commit v4 on v3

--- a/solution.py
+++ b/solution.py
@@ -284,9 +284,9 @@
     agg = jnp.arange(rows, dtype=jnp.int32)[:, None] // AGG
     seg = agg * 9 + where_u * 3 + where_r // AGG - agg + 1
     meta = jnp.concatenate([where_u * rows + where_r + 64 * seg, p_cells], axis=1).reshape(rows * 8)
-    everyone = lax.all_to_all(
-        jnp.broadcast_to(meta[None], (cells, rows * 8)), ("z", "y"), 0, 0, tiled=True
-    )
+    spread = jnp.broadcast_to(meta[None], (cells, rows * 8))
+    spread, *beside = lax.optimization_barrier((spread, *p_ring[1]))
+    everyone = lax.all_to_all(spread, ("z", "y"), 0, 0, tiled=True)
     mb, ma = shifted(everyone)
     three = jnp.stack([mb, everyone, ma]).reshape(-1)
     flat = everyone.reshape(-1)
@@ -309,7 +309,7 @@
         groups.append(((-d, d), ((0, *whole), (1, *whole)), a_ring[d], p_ring[d], d - 1, 0))
     groups.append(((half,), ((0, 0, mid), (0, mid, mid)), a_ring[half], p_ring[half], 2, 2))
     batches = [
-        (p_blocks,) + p_ring[1],
+        (p_blocks, *beside),
         p_ring[2],
         p_ring[3] + p_ring[4],
     ]

time: 187 us -> 186 us (level)
  starting transfers between devices: 70.5 us -> 67.4 us
    all_to_all x1, starting transfers between devices: 8.86 us -> 5.75 us  [local(): everyone = lax.all_to_all(spread, ('z', 'y'), 0, 0, tiled=True)]
    ppermute x7, starting transfers between devices: 18.8 us -> 20.7 us  [turned(): down = lax.ppermute(down, 'z', [((i + 1) % n, i) for i in range(n)])]
    ppermute x8, starting transfers between devices: 5.66 us -> 3.75 us  [turned(): up = lax.ppermute(up, 'z', [(i, (i + 1) % n) for i in range(n)])]
  transfers between devices with their start and end apart: 30 -> 30, of which waited for: 9 -> 10; matrix products, arithmetic and copies ran while one was open for 5% -> 5% of each run, Pallas kernels for 14% -> 14%
where the time goes in v4:
time: 186 us; the launch traced here: 184 us
  starting transfers between devices  67.4 us (36%)
  waiting for transfers between devices  58.6 us (32%)
  Pallas kernels  44.5 us (24%)
  local copies, waits for them, and re-layouts  11.2 us (6%)
  other arithmetic  2.23 us (1%)
    ppermute x8, waiting for transfers between devices, turned(): up = lax.ppermute(up, 'z', [(i, (i + 1) % n) for i in range(n)])  40.5 us
    ppermute x7, starting transfers between devices, turned(): down = lax.ppermute(down, 'z', [((i + 1) % n, i) for i in range(n)])  20.7 us
    pallas_call x4, Pallas kernels, local(): pl.pallas_call(functools.partial(term_kernel, rows, nnz_a, nz, ny, offset...  20.6 us
    all_to_all x3, starting transfers between devices, local(): got.append(lax.all_to_all(sent, 'y', 0, 0, tiled=True))  13.7 us
    pallas_call x1, Pallas kernels, local(): pl.pallas_call(functools.partial(last_kernel, nseg, nz, ny, nnz_a, offset...  12.5 us
    pallas_call x1, Pallas kernels, local(): pl.pallas_call(functools.partial(add_kernel, nseg, nz, ny, nnz_a, offsets...  11.4 us
    all_to_all x1, waiting for transfers between devices, local(): everyone = lax.all_to_all(spread, ('z', 'y'), 0, 0, tiled=True)  9.69 us
    ppermute x4, starting transfers between devices, shifted(): before = lax.ppermute(value, 'frame', [(i, i + 1) for i in range(n - 1)])  9.63 us
  transfers between devices with their start and end apart: 30, of which 10 were waited for; matrix products, arithmetic and copies ran while one was open for 5% of the time, Pallas kernels for 14%

profile of v4, /device:TPU:2, one launch (start us, length us, event | category | flops | bytes accessed | tf_op | source)
XLA Modules:
  0.0 184.5 jit_solution(1582230543232897996)
XLA Ops:
  0.0 5.9 %collective-permute-start.1 = (bf16[16,64,128]{2,1,0:T(8,128)(2,1)}, bf16[16,64,128]{2,1,0:T(8,128)(2,1)S(1)}, u32[]{:S(2)}, u32[]{:S(2)}) collective-permute-start(bf16[16,64,128]{2,1,0:T(8,128)(2,1)} %refs_3_.1), channel_id=1, source_target_pairs={{4,0},{8,4},{12,8},{16,12},{20,16},{24,20},{28,24},{0,28},{5,1},{9... | collective-permute-start | bytes 786440 | tf_op jit(solution)/shard_map/ppermute | solution.py:30
  5.9 3.3 %collective-permute-start.11 = (bf16[16,64,384]{2,1,0:T(8,128)(2,1)}, bf16[16,64,384]{2,1,0:T(8,128)(2,1)S(1)}, u32[]{:S(2)}, u32[]{:S(2)}) collective-permute-start(bf16[16,64,384]{2,1,0:T(8,128)(2,1)} %refs_0_.1), channel_id=1, source_target_pairs={{4,0},{8,4},{12,8},{16,12},{20,16},{24,20},{28,24},{0,28},{5,1},{9... | collective-permute-start | bytes 2359304 | tf_op jit(solution)/shard_map/ppermute | solution.py:30
  12.9 3.6 %collective-permute-done.refs_4_ = bf16[16,64,128]{2,1,0:T(8,128)(2,1)S(1)} collective-permute-done((bf16[16,64,128]{2,1,0:T(8,128)(2,1)}, bf16[16,64,128]{2,1,0:T(8,128)(2,1)S(1)}, u32[]{:S(2)}, u32[]{:S(2)}) %collective-permute-start) | collective-permute-done | bytes 262176 | tf_op jit(solution)/shard_map/ppermute | solution.py:27
  22.8 5.8 %all-to-all-start = ((s32[32,1,128]{2,1,0:T(1,128)}), s32[32,1,128]{2,1,0:T(1,128)S(1)}, u32[]{:S(2)}, u32[]{:S(2)}) async-start(s32[32,1,128]{2,1,0:T(1,128)} %bitcast), calls=%async_computation | async-start | bytes 32768 | tf_op jit(solution)/shard_map/all_to_all | solution.py:289
  28.7 9.7 %all-to-all-done = s32[32,1,128]{2,1,0:T(1,128)S(1)} async-done(((s32[32,1,128]{2,1,0:T(1,128)}), s32[32,1,128]{2,1,0:T(1,128)S(1)}, u32[]{:S(2)}, u32[]{:S(2)}) %all-to-all-start) | async-done | bytes 16416 | tf_op jit(solution)/shard_map/all_to_all | solution.py:289
  40.5 6.0 %terms.5 = bf16[24,64,768]{2,1,0:T(8,128)(2,1)} custom-call(s32[4096]{0:T(1024)S(1)} %bitcast.19, s32[2]{0:T(128)S(1)} %pad_add_fusion.3.here, bf16[16,64,384]{2,1,0:T(8,128)(2,1)S(1)} %copy-done.5, bf16[16,64,384]{2,1,0:T(8,128)(2,1)S(1)} %collective-permute-done.9.refs_1_, bf16[16,64,384]{2,1,0:T(8,128)(2,1)S(1)} %collective-permute-done.11.refs_2_, ...), custom_call_target="tpu_custom_call" | custom-call | tf_op jit(solution)/shard_map/terms/pallas_call | solution.py:333
  46.5 4.5 %all-to-all-start.1 = ((bf16[4,6,64,768]{3,2,1,0:T(8,128)(2,1)}), bf16[4,6,64,768]{3,2,1,0:T(8,128)(2,1)}, u32[]{:S(2)}, u32[]{:S(2)}) async-start(bf16[4,6,64,768]{3,2,1,0:T(8,128)(2,1)} %bitcast.13), calls=%async_computation.1 | async-start | bytes 4718592 | tf_op jit(solution)/shard_map/all_to_all | solution.py:327
  51.8 2.6 %collective-permute-start.6 = (bf16[16,64,128]{2,1,0:T(8,128)(2,1)S(1)}, bf16[16,64,128]{2,1,0:T(8,128)(2,1)S(1)}, u32[]{:S(2)}, u32[]{:S(2)}) collective-permute-start(bf16[16,64,128]{2,1,0:T(8,128)(2,1)S(1)} %collective-permute-done.1.refs_5_), channel_id=1, source_target_pairs={{4,0},{8,4},{12,8},{16,12},{20,16},{24,20},{28,24},{0,28},{5,1},{9... | collective-permute-start | bytes 786440 | tf_op jit(solution)/shard_map/ppermute | solution.py:30
  54.4 5.7 %collective-permute-done.4.refs_2_ = bf16[16,64,128]{2,1,0:T(8,128)(2,1)S(1)} collective-permute-done((bf16[16,64,128]{2,1,0:T(8,128)(2,1)S(1)}, bf16[16,64,128]{2,1,0:T(8,128)(2,1)S(1)}, u32[]{:S(2)}, u32[]{:S(2)}) %collective-permute-start.4) | collective-permute-done | bytes 262176 | tf_op jit(solution)/shard_map/ppermute | solution.py:27
  60.2 3.2 %collective-permute-start.12 = (bf16[16,64,384]{2,1,0:T(8,128)(2,1)S(1)}, bf16[16,64,384]{2,1,0:T(8,128)(2,1)S(1)}, u32[]{:S(2)}, u32[]{:S(2)}) collective-permute-start(bf16[16,64,384]{2,1,0:T(8,128)(2,1)S(1)} %collective-permute-done.11.refs_2_), channel_id=1, source_target_pairs={{4,0},{8,4},{12,8},{16,12},{20,16},{24,20},{28,24},{0,28},{5,1},{9... | collective-permute-start | bytes 2359304 | tf_op jit(solution)/shard_map/ppermute | solution.py:30
  67.9 17.3 %collective-permute-done.5.refs_2_ = bf16[16,64,128]{2,1,0:T(8,128)(2,1)S(1)} collective-permute-done((bf16[16,64,128]{2,1,0:T(8,128)(2,1)S(1)}, bf16[16,64,128]{2,1,0:T(8,128)(2,1)S(1)}, u32[]{:S(2)}, u32[]{:S(2)}) %collective-permute-start.5) | collective-permute-done | bytes 262176 | tf_op jit(solution)/shard_map/ppermute | solution.py:27
  87.3 5.3 %terms.4 = bf16[16,64,768]{2,1,0:T(8,128)(2,1)} custom-call(s32[4096]{0:T(1024)S(1)} %bitcast.20, s32[2]{0:T(128)S(1)} %pad_add_fusion.3.here, bf16[16,64,384]{2,1,0:T(8,128)(2,1)} %collective-permute-done.10.refs_0_, bf16[16,64,384]{2,1,0:T(8,128)(2,1)S(1)} %collective-permute-done.12.refs_1_, bf16[16,64,128]{2,1,0:T(8,128)(2,1)S(1)} %collective-permute-done.4.refs_2_, ...), custom_call_target="tpu_custom_call" | custom-call | tf_op jit(solution)/shard_map/terms/pallas_call | solution.py:333
  92.9 4.4 %all-to-all-start.2 = ((bf16[4,4,64,768]{3,2,1,0:T(8,128)(2,1)}), bf16[4,4,64,768]{3,2,1,0:T(8,128)(2,1)}, u32[]{:S(2)}, u32[]{:S(2)}) async-start(bf16[4,4,64,768]{3,2,1,0:T(8,128)(2,1)} %bitcast.12), calls=%async_computation.2 | async-start | bytes 3145728 | tf_op jit(solution)/shard_map/all_to_all | solution.py:327
  102.7 2.6 %collective-permute-start.18 = (bf16[16,64,384]{2,1,0:T(8,128)(2,1)}, bf16[16,64,384]{2,1,0:T(8,128)(2,1)S(1)}, u32[]{:S(2)}, u32[]{:S(2)}) collective-permute-start(bf16[16,64,384]{2,1,0:T(8,128)(2,1)} %copy-done.6), channel_id=1, source_target_pairs={{4,0},{8,4},{12,8},{16,12},{20,16},{24,20},{28,24},{0,28},{5,1},{9... | collective-permute-start | bytes 2359304 | tf_op jit(solution)/shard_map/ppermute | solution.py:30
  105.3 10.1 %collective-permute-done.17.refs_0_ = bf16[16,64,384]{2,1,0:T(8,128)(2,1)S(1)} collective-permute-done((bf16[16,64,384]{2,1,0:T(8,128)(2,1)}, bf16[16,64,384]{2,1,0:T(8,128)(2,1)S(1)}, u32[]{:S(2)}, u32[]{:S(2)}) %collective-permute-start.17) | collective-permute-done | bytes 786464 | tf_op jit(solution)/shard_map/ppermute | solution.py:27
  115.4 7.7 %collective-permute-done.18.refs_1_ = bf16[16,64,384]{2,1,0:T(8,128)(2,1)S(1)} collective-permute-done((bf16[16,64,384]{2,1,0:T(8,128)(2,1)}, bf16[16,64,384]{2,1,0:T(8,128)(2,1)S(1)}, u32[]{:S(2)}, u32[]{:S(2)}) %collective-permute-start.18) | collective-permute-done | bytes 786464 | tf_op jit(solution)/shard_map/ppermute | solution.py:30
  125.0 5.0 %terms.6 = bf16[16,64,768]{2,1,0:T(8,128)(2,1)} custom-call(s32[4096]{0:T(1024)S(1)} %bitcast.21, s32[2]{0:T(128)S(1)} %pad_add_fusion.3.here, bf16[16,64,384]{2,1,0:T(8,128)(2,1)S(1)} %collective-permute-done.17.refs_0_, bf16[16,64,384]{2,1,0:T(8,128)(2,1)S(1)} %collective-permute-done.18.refs_1_, bf16[16,64,128]{2,1,0:T(8,128)(2,1)S(1)} %copy-done.2, ...), custom_call_target="tpu_custom_call" | custom-call | tf_op jit(solution)/shard_map/terms/pallas_call | solution.py:333
  130.0 4.8 %all-to-all-start.3 = ((bf16[4,4,64,768]{3,2,1,0:T(8,128)(2,1)}), bf16[4,4,64,768]{3,2,1,0:T(8,128)(2,1)}, u32[]{:S(2)}, u32[]{:S(2)}) async-start(bf16[4,4,64,768]{3,2,1,0:T(8,128)(2,1)} %bitcast.14), calls=%async_computation.3 | async-start | bytes 3145728 | tf_op jit(solution)/shard_map/all_to_all | solution.py:327
  136.4 3.2 %collective-permute-start.22 = (bf16[8,64,384]{2,1,0:T(8,128)(2,1)}, bf16[8,64,384]{2,1,0:T(8,128)(2,1)S(1)}, u32[]{:S(2)}, u32[]{:S(2)}) collective-permute-start(bf16[8,64,384]{2,1,0:T(8,128)(2,1)} %slice.14), channel_id=1, source_target_pairs={{4,0},{8,4},{12,8},{16,12},{20,16},{24,20},{28,24},{0,28},{5,1},{9... | collective-permute-start | bytes 1179656 | tf_op jit(solution)/shard_map/ppermute | solution.py:30
  144.2 3.5 %collective-permute-done.21.refs_0_ = bf16[8,64,384]{2,1,0:T(8,128)(2,1)S(1)} collective-permute-done((bf16[8,64,384]{2,1,0:T(8,128)(2,1)}, bf16[8,64,384]{2,1,0:T(8,128)(2,1)S(1)}, u32[]{:S(2)}, u32[]{:S(2)}) %collective-permute-start.21) | collective-permute-done | bytes 393248 | tf_op jit(solution)/shard_map/ppermute | solution.py:27
  147.8 4.4 %terms.7 = (bf16[2,64,768]{2,1,0:T(8,128)(2,1)S(1)}, bf16[2,64,768]{2,1,0:T(8,128)(2,1)S(1)}, bf16[2,64,768]{2,1,0:T(8,128)(2,1)S(1)}, bf16[2,64,768]{2,1,0:T(8,128)(2,1)S(1)}) custom-call(s32[4096]{0:T(1024)S(1)} %bitcast.24, s32[2]{0:T(128)S(1)} %pad_add_fusion.3.here, bf16[8,64,384]{2,1,0:T(8,128)(2,1)S(1)} %collective-permute-done.21.refs_0_, ...), custom_call_target="tpu_custom_call" | custom-call | tf_op jit(solution)/shard_map/terms/pallas_call | solution.py:333
  154.0 2.8 %collective-permute-start.24 = (bf16[2,64,768]{2,1,0:T(8,128)(2,1)S(1)}, bf16[2,64,768]{2,1,0:T(8,128)(2,1)S(1)}, u32[]{:S(2)}, u32[]{:S(2)}) collective-permute-start(bf16[2,64,768]{2,1,0:T(8,128)(2,1)S(1)} %get-tuple-element.33), channel_id=1, source_target_pairs={{0,2},{1,3},{2,0},{3,1},{4,6},{5,7},{6,4},{7,5},{8,10},{9,11},{10,... | collective-permute-start | bytes 589832 | tf_op jit(solution)/shard_map/ppermute | solution.py:357
  159.6 11.4 %add.81.part = f32[18,64,2048]{2,1,0:T(8,128)} custom-call(s32[12288]{0:T(1024)} %bitcast.26, s32[64]{0:T(128)} %reshape.109.slots, s32[2]{0:T(128)} %copy-done.8, bf16[4,6,64,768]{3,2,1,0:T(8,128)(2,1)} %all-to-all-done.1.refs_0_, bf16[4,4,64,768]{3,2,1,0:T(8,128)(2,1)} %all-to-all-done.2.refs_1_), custom_call_target="tpu_custom_call" | custom-call | tf_op jit(solution)/shard_map/add/pallas_call | solution.py:361
  171.9 12.5 %finish.1 = bf16[18,64,2048]{2,1,0:T(8,128)(2,1)} custom-call(s32[12288]{0:T(1024)} %bitcast.27, s32[64]{0:T(128)} %reshape.109.slots, s32[2]{0:T(128)} %copy-done.8, f32[18,64,2048]{2,1,0:T(8,128)} %add.81.part, bf16[4,4,64,768]{3,2,1,0:T(8,128)(2,1)} %all-to-all-done.3.got, bf16[2,64,768]{2,1,0:T(8,128)(2,1)} %copy-done.7, bf16[2,64,768]{2,1,0:T(8,128)(2,1)} %copy-done.9, ...), custom_call_target="tpu_custom_call" | custom-call | tf_op jit(solution)/shard_map/finish/pallas_call | solution.py:376
  (91 shorter events, 39.0 us)
Async XLA Ops:
  0.0 12.9 %collective-permute-start.1 = (bf16[16,64,128]{2,1,0:T(8,128)(2,1)}, bf16[16,64,128]{2,1,0:T(8,128)(2,1)S(1)}, u32[]{:S(2)}, u32[]{:S(2)}) collective-permute-start(bf16[16,64,128]{2,1,0:T(8,128)(2,1)} %refs_3_.1), channel_id=1, source_target_pairs={{4,0},{8,4},{12,8},{16,12},{20,16},{24,20},{28,24},{0,28},{5,1},{9... | collective-permute-start | bytes 786440 | tf_op jit(solution)/shard_map/ppermute | solution.py:30
  5.9 32.5 %collective-permute-start.9 = (bf16[16,64,384]{2,1,0:T(8,128)(2,1)}, bf16[16,64,384]{2,1,0:T(8,128)(2,1)S(1)}, u32[]{:S(2)}, u32[]{:S(2)}) collective-permute-start(bf16[16,64,384]{2,1,0:T(8,128)(2,1)} %refs_0_.1), channel_id=1, source_target_pairs={{0,4},{4,8},{8,12},{12,16},{16,20},{20,24},{24,28},{28,0},{1,5},{5... | collective-permute-start | bytes 2359304 | tf_op jit(solution)/shard_map/ppermute | solution.py:27
  5.9 32.5 %collective-permute-start.11 = (bf16[16,64,384]{2,1,0:T(8,128)(2,1)}, bf16[16,64,384]{2,1,0:T(8,128)(2,1)S(1)}, u32[]{:S(2)}, u32[]{:S(2)}) collective-permute-start(bf16[16,64,384]{2,1,0:T(8,128)(2,1)} %refs_0_.1), channel_id=1, source_target_pairs={{4,0},{8,4},{12,8},{16,12},{20,16},{24,20},{28,24},{0,28},{5,1},{9... | collective-permute-start | bytes 2359304 | tf_op jit(solution)/shard_map/ppermute | solution.py:30
  18.5 19.9 %collective-permute-start.16 = (bf16[48,64,128]{2,1,0:T(8,128)(2,1)}, bf16[48,64,128]{2,1,0:T(8,128)(2,1)S(1)}, u32[]{:S(2)}, u32[]{:S(2)}) collective-permute-start(bf16[48,64,128]{2,1,0:T(8,128)(2,1)} %constant_dynamic-update-slice_fusion.2), channel_id=1, source_target_pairs={{32,0},{64,32},{96,64},{128,96},{160,128},{192,160},{224,192},{33,... | collective-permute-start | bytes 2359304 | tf_op jit(solution)/shard_map/ppermute | solution.py:21
  20.4 18.0 %collective-permute-start.15 = (bf16[48,64,128]{2,1,0:T(8,128)(2,1)}, bf16[48,64,128]{2,1,0:T(8,128)(2,1)}, u32[]{:S(2)}, u32[]{:S(2)}) collective-permute-start(bf16[48,64,128]{2,1,0:T(8,128)(2,1)} %constant_dynamic-update-slice_fusion.2), channel_id=1, source_target_pairs={{0,32},{32,64},{64,96},{96,128},{128,160},{160,192},{192,224},{1,3... | collective-permute-start | bytes 2359304 | tf_op jit(solution)/shard_map/ppermute | solution.py:20
  22.8 15.5 %all-to-all-start = ((s32[32,1,128]{2,1,0:T(1,128)}), s32[32,1,128]{2,1,0:T(1,128)S(1)}, u32[]{:S(2)}, u32[]{:S(2)}) async-start(s32[32,1,128]{2,1,0:T(1,128)} %bitcast), calls=%async_computation | async-start | bytes 32768 | tf_op jit(solution)/shard_map/all_to_all | solution.py:289
  46.5 46.4 %all-to-all-start.1 = ((bf16[4,6,64,768]{3,2,1,0:T(8,128)(2,1)}), bf16[4,6,64,768]{3,2,1,0:T(8,128)(2,1)}, u32[]{:S(2)}, u32[]{:S(2)}) async-start(bf16[4,6,64,768]{3,2,1,0:T(8,128)(2,1)} %bitcast.13), calls=%async_computation.1 | async-start | bytes 4718592 | tf_op jit(solution)/shard_map/all_to_all | solution.py:327
  60.1 27.2 %collective-permute-start.10 = (bf16[16,64,384]{2,1,0:T(8,128)(2,1)S(1)}, bf16[16,64,384]{2,1,0:T(8,128)(2,1)}, u32[]{:S(2)}, u32[]{:S(2)}) collective-permute-start(bf16[16,64,384]{2,1,0:T(8,128)(2,1)S(1)} %collective-permute-done.9.refs_1_), channel_id=1, source_target_pairs={{0,4},{4,8},{8,12},{12,16},{16,20},{20,24},{24,28},{28,0},{1,5},{5... | collective-permute-start | bytes 2359304 | tf_op jit(solution)/shard_map/ppermute | solution.py:27
  60.2 27.1 %collective-permute-start.12 = (bf16[16,64,384]{2,1,0:T(8,128)(2,1)S(1)}, bf16[16,64,384]{2,1,0:T(8,128)(2,1)S(1)}, u32[]{:S(2)}, u32[]{:S(2)}) collective-permute-start(bf16[16,64,384]{2,1,0:T(8,128)(2,1)S(1)} %collective-permute-done.11.refs_2_), channel_id=1, source_target_pairs={{4,0},{8,4},{12,8},{16,12},{20,16},{24,20},{28,24},{0,28},{5,1},{9... | collective-permute-start | bytes 2359304 | tf_op jit(solution)/shard_map/ppermute | solution.py:30
  63.4 21.8 %collective-permute-start.14 = (bf16[32,64,128]{2,1,0:T(8,128)(2,1)S(1)}, bf16[32,64,128]{2,1,0:T(8,128)(2,1)S(1)}, u32[]{:S(2)}, u32[]{:S(2)}) collective-permute-start(bf16[32,64,128]{2,1,0:T(8,128)(2,1)S(1)} %constant_dynamic-update-slice_fusion), channel_id=1, source_target_pairs={{32,0},{64,32},{96,64},{128,96},{160,128},{192,160},{224,192},{33,... | collective-permute-start | bytes 1572872 | tf_op jit(solution)/shard_map/ppermute | solution.py:21
  65.4 21.9 %collective-permute-start.13 = (bf16[32,64,128]{2,1,0:T(8,128)(2,1)S(1)}, bf16[32,64,128]{2,1,0:T(8,128)(2,1)S(1)}, u32[]{:S(2)}, u32[]{:S(2)}) collective-permute-start(bf16[32,64,128]{2,1,0:T(8,128)(2,1)S(1)} %constant_dynamic-update-slice_fusion), channel_id=1, source_target_pairs={{0,32},{32,64},{64,96},{96,128},{128,160},{160,192},{192,224},{1,3... | collective-permute-start | bytes 1572872 | tf_op jit(solution)/shard_map/ppermute | solution.py:20
  67.8 17.4 %collective-permute-start.5 = (bf16[16,64,128]{2,1,0:T(8,128)(2,1)S(1)}, bf16[16,64,128]{2,1,0:T(8,128)(2,1)S(1)}, u32[]{:S(2)}, u32[]{:S(2)}) collective-permute-start(bf16[16,64,128]{2,1,0:T(8,128)(2,1)S(1)} %collective-permute-done.4.refs_2_), channel_id=1, source_target_pairs={{0,4},{4,8},{8,12},{12,16},{16,20},{20,24},{24,28},{28,0},{1,5},{5... | collective-permute-start | bytes 786440 | tf_op jit(solution)/shard_map/ppermute | solution.py:27
  92.9 37.1 %all-to-all-start.2 = ((bf16[4,4,64,768]{3,2,1,0:T(8,128)(2,1)}), bf16[4,4,64,768]{3,2,1,0:T(8,128)(2,1)}, u32[]{:S(2)}, u32[]{:S(2)}) async-start(bf16[4,4,64,768]{3,2,1,0:T(8,128)(2,1)} %bitcast.12), calls=%async_computation.2 | async-start | bytes 3145728 | tf_op jit(solution)/shard_map/all_to_all | solution.py:327
  97.4 18.0 %collective-permute-start.17 = (bf16[16,64,384]{2,1,0:T(8,128)(2,1)}, bf16[16,64,384]{2,1,0:T(8,128)(2,1)S(1)}, u32[]{:S(2)}, u32[]{:S(2)}) collective-permute-start(bf16[16,64,384]{2,1,0:T(8,128)(2,1)} %collective-permute-done.10.refs_0_), channel_id=1, source_target_pairs={{0,4},{4,8},{8,12},{12,16},{16,20},{20,24},{24,28},{28,0},{1,5},{5... | collective-permute-start | bytes 2359304 | tf_op jit(solution)/shard_map/ppermute | solution.py:27
  98.2 17.2 %collective-permute-start.20 = (bf16[48,64,128]{2,1,0:T(8,128)(2,1)S(1)}, bf16[48,64,128]{2,1,0:T(8,128)(2,1)S(1)}, u32[]{:S(2)}, u32[]{:S(2)}) collective-permute-start(bf16[48,64,128]{2,1,0:T(8,128)(2,1)S(1)} %constant_dynamic-update-slice_fusion.5), channel_id=1, source_target_pairs={{32,0},{64,32},{96,64},{128,96},{160,128},{192,160},{224,192},{33,... | collective-permute-start | bytes 2359304 | tf_op jit(solution)/shard_map/ppermute | solution.py:21
  100.3 15.1 %collective-permute-start.19 = (bf16[48,64,128]{2,1,0:T(8,128)(2,1)S(1)}, bf16[48,64,128]{2,1,0:T(8,128)(2,1)S(1)}, u32[]{:S(2)}, u32[]{:S(2)}) collective-permute-start(bf16[48,64,128]{2,1,0:T(8,128)(2,1)S(1)} %constant_dynamic-update-slice_fusion.5), channel_id=1, source_target_pairs={{0,32},{32,64},{64,96},{96,128},{128,160},{160,192},{192,224},{1,3... | collective-permute-start | bytes 2359304 | tf_op jit(solution)/shard_map/ppermute | solution.py:20
  102.7 20.4 %collective-permute-start.18 = (bf16[16,64,384]{2,1,0:T(8,128)(2,1)}, bf16[16,64,384]{2,1,0:T(8,128)(2,1)S(1)}, u32[]{:S(2)}, u32[]{:S(2)}) collective-permute-start(bf16[16,64,384]{2,1,0:T(8,128)(2,1)} %copy-done.6), channel_id=1, source_target_pairs={{4,0},{8,4},{12,8},{16,12},{20,16},{24,20},{28,24},{0,28},{5,1},{9... | collective-permute-start | bytes 2359304 | tf_op jit(solution)/shard_map/ppermute | solution.py:30
  130.0 41.1 %all-to-all-start.3 = ((bf16[4,4,64,768]{3,2,1,0:T(8,128)(2,1)}), bf16[4,4,64,768]{3,2,1,0:T(8,128)(2,1)}, u32[]{:S(2)}, u32[]{:S(2)}) async-start(bf16[4,4,64,768]{3,2,1,0:T(8,128)(2,1)} %bitcast.14), calls=%async_computation.3 | async-start | bytes 3145728 | tf_op jit(solution)/shard_map/all_to_all | solution.py:327
  135.5 12.1 %collective-permute-start.21 = (bf16[8,64,384]{2,1,0:T(8,128)(2,1)}, bf16[8,64,384]{2,1,0:T(8,128)(2,1)S(1)}, u32[]{:S(2)}, u32[]{:S(2)}) collective-permute-start(bf16[8,64,384]{2,1,0:T(8,128)(2,1)} %slice.13), channel_id=1, source_target_pairs={{0,4},{4,8},{8,12},{12,16},{16,20},{20,24},{24,28},{28,0},{1,5},{5... | collective-permute-start | bytes 1179656 | tf_op jit(solution)/shard_map/ppermute | solution.py:27
  139.6 19.4 %collective-permute-start.3 = (s32[32,128]{1,0:T(8,128)S(1)}, s32[32,128]{1,0:T(8,128)S(1)}, u32[]{:S(2)}, u32[]{:S(2)}) collective-permute-start(s32[32,128]{1,0:T(8,128)S(1)} %bitcast.22), channel_id=1, source_target_pairs={{32,0},{64,32},{96,64},{128,96},{160,128},{192,160},{224,192},{33,... | collective-permute-start | bytes 49160 | tf_op jit(solution)/shard_map/ppermute | solution.py:21
  141.5 17.5 %collective-permute-start.2 = (s32[32,128]{1,0:T(8,128)S(1)}, s32[32,128]{1,0:T(8,128)S(1)}, u32[]{:S(2)}, u32[]{:S(2)}) collective-permute-start(s32[32,128]{1,0:T(8,128)S(1)} %bitcast.23), channel_id=1, source_target_pairs={{0,32},{32,64},{64,96},{96,128},{128,160},{160,192},{192,224},{1,3... | collective-permute-start | bytes 49160 | tf_op jit(solution)/shard_map/ppermute | solution.py:20
  152.2 18.8 %collective-permute-start.23 = (bf16[2,64,768]{2,1,0:T(8,128)(2,1)S(1)}, bf16[2,64,768]{2,1,0:T(8,128)(2,1)S(1)}, u32[]{:S(2)}, u32[]{:S(2)}) collective-permute-start(bf16[2,64,768]{2,1,0:T(8,128)(2,1)S(1)} %get-tuple-element.32), channel_id=1, source_target_pairs={{0,1},{1,2},{2,3},{3,0},{4,5},{5,6},{6,7},{7,4},{8,9},{9,10},{10,1... | collective-permute-start | bytes 589832 | tf_op jit(solution)/shard_map/ppermute | solution.py:357
  154.0 17.0 %collective-permute-start.24 = (bf16[2,64,768]{2,1,0:T(8,128)(2,1)S(1)}, bf16[2,64,768]{2,1,0:T(8,128)(2,1)S(1)}, u32[]{:S(2)}, u32[]{:S(2)}) collective-permute-start(bf16[2,64,768]{2,1,0:T(8,128)(2,1)S(1)} %get-tuple-element.33), channel_id=1, source_target_pairs={{0,2},{1,3},{2,0},{3,1},{4,6},{5,7},{6,4},{7,5},{8,10},{9,11},{10,... | collective-permute-start | bytes 589832 | tf_op jit(solution)/shard_map/ppermute | solution.py:357
  156.8 14.2 %collective-permute-start.25 = (bf16[2,64,768]{2,1,0:T(8,128)(2,1)S(1)}, bf16[2,64,768]{2,1,0:T(8,128)(2,1)S(1)}, u32[]{:S(2)}, u32[]{:S(2)}) collective-permute-start(bf16[2,64,768]{2,1,0:T(8,128)(2,1)S(1)} %get-tuple-element.34), channel_id=1, source_target_pairs={{0,3},{1,0},{2,1},{3,2},{4,7},{5,4},{6,5},{7,6},{8,11},{9,8},{10,9... | collective-permute-start | bytes 589832 | tf_op jit(solution)/shard_map/ppermute | solution.py:357
  (18 other events, 231.7 us)
